TPU v7x, 512 devices: a whole 4x4x16 slice. The times are simulated.
512 devices in a mesh: depth: 16 (over x, y), trans: 32 (over z, core).
Axes of the slice: x: 4, y: 4, z: 16, core: 2. Of those that a mesh axis runs over, the one named last changes fastest.
Arguments:
- flight_fields: bfloat16 [16, 2, 2, 1024, 1024], P('depth', None, None, 'trans'), may hold values from -6 to 6
- top_fields: bfloat16 [2, 2, 1024, 1024], P(None, None, 'trans'), may hold values from -6 to 6
- slowness: float32 [16, 1024, 1024], P('depth', 'trans'), may hold values from 0.5 to 1.5
- ref_slowness: float32 [16], P('depth'), may hold values from 0.6 to 1
- flight_blocks: int32 [16], replicated, may hold values from 128 to 191
- top_block: int32 [1], replicated, may hold values from 0 to 255
Outputs:
- image: float32 [16, 1024, 1024], P('depth', 'trans')
- next_fields: bfloat16 [16, 2, 2, 1024, 1024], P('depth', None, None, 'trans')
All inputs are finite; a program needn't handle non-finite values.
Results may differ from a plain program's by a relative error of at most 0.02.
Values may be sent and summed in bfloat16 or wider, within the bound.
A program may use at most 64 MiB of HBM per device.

v0:
```python
import math

import jax
import jax.numpy as jnp
from jax import lax
from jax.sharding import PartitionSpec as P

NX = 1024
NY = 1024
NFREQ = 256


omega_top = 4.0
step_length = 0.5


def passed_along(value, axis, steps):
    count = lax.axis_size(axis)
    leading, last = (max(0, -steps), min(count, count - steps))
    return lax.ppermute(value, axis, [(source, source + steps) for source in range(leading, last)])


def make_table(length):
    positions = jnp.arange(length, dtype=jnp.int32)
    product = positions[:, None] * positions[None, :] % length
    angles = product.astype(jnp.float32) * (2.0 * math.pi / length)
    scaling = 1.0 / math.sqrt(length)
    return (jnp.concatenate([jnp.cos(angles), jnp.sin(angles)], axis=1) * scaling).astype(
        jnp.bfloat16
    )


def wavenumber(positions, length):
    signed = jnp.where(positions < length // 2, positions, positions - length)
    return signed.astype(jnp.float32) * (2.0 * math.pi / length)


def mix(product, along, half_size, orient):
    cosine_part = lax.slice_in_dim(product, 0, half_size, axis=along)
    sine_part = lax.slice_in_dim(product, half_size, 2 * half_size, axis=along)
    real_part = cosine_part[:, 0] + orient * sine_part[:, 1]
    imag_part = cosine_part[:, 1] - orient * sine_part[:, 0]
    return jnp.stack([real_part, imag_part], axis=1)


def rotate(values, cosines, sine_vals):
    real_part = values[:, 0] * cosines - values[:, 1] * sine_vals
    imag_part = values[:, 0] * sine_vals + values[:, 1] * cosines
    return jnp.stack([real_part, imag_part], axis=1)


def spectral(angular, reference_s, wave_x, wave_y):
    quad = (angular * reference_s) ** 2 - wave_x * wave_x - wave_y * wave_y
    travel = jnp.sqrt(jnp.maximum(quad, 0.0)) * step_length
    damping = jnp.exp(-jnp.sqrt(jnp.maximum(-quad, 0.0)) * step_length)
    cosines = damping * jnp.cos(travel)
    sine_vals = damping * jnp.sin(travel)
    return (jnp.stack([cosines, cosines]), jnp.stack([sine_vals, -sine_vals]))


def propagate(fields, spec_cos, spec_sin, space_cos, space_sin, to_cols, to_rows, table_x, table_y):
    length_y = table_y.shape[0]
    length_x = table_x.shape[0]
    product = jnp.einsum("fcry,yk->fckr", fields, table_y, preferred_element_type=jnp.float32)
    first = mix(product, 2, length_y, 1.0).astype(jnp.bfloat16)
    columns = to_cols(first)
    product = jnp.dot(columns, table_x, preferred_element_type=jnp.float32)
    spectrum = mix(product, 3, length_x, 1.0)
    shifted = rotate(spectrum, spec_cos, spec_sin).astype(jnp.bfloat16)
    product = jnp.dot(shifted, table_x, preferred_element_type=jnp.float32)
    back_x = mix(product, 3, length_x, -1.0).astype(jnp.bfloat16)
    rows_back = to_rows(back_x)
    product = jnp.einsum("fckr,ky->fcry", rows_back, table_y, preferred_element_type=jnp.float32)
    space = mix(product, 3, length_y, -1.0)
    return rotate(space, space_cos, space_sin).astype(jnp.bfloat16)


def together_cols(values):
    return lax.all_to_all(values, "trans", split_axis=2, concat_axis=3, tiled=True)


def together_rows(values):
    return lax.all_to_all(values, "trans", split_axis=3, concat_axis=2, tiled=True)


def advance(fields, block_id, slowness, ref_slowness, table_x, table_y):
    length_x = table_x.shape[0]
    length_y = table_y.shape[0]
    trans_count = lax.axis_size("trans")
    local_ky = length_y // trans_count
    ky_rows = lax.axis_index("trans") * local_ky + jnp.arange(local_ky, dtype=jnp.int32)
    wave_y = wavenumber(ky_rows, length_y)[:, None]
    wave_x = wavenumber(jnp.arange(length_x, dtype=jnp.int32), length_x)[None, :]
    angular = omega_top * (block_id.astype(jnp.float32) + 1.0) / NFREQ
    reference_s = ref_slowness[0]
    spec_cos, spec_sin = spectral(angular, reference_s, wave_x, wave_y)
    rotation = angular * (slowness[0] - reference_s) * step_length
    cos_r = jnp.cos(rotation)
    sin_r = jnp.sin(rotation)
    space_cos = jnp.stack([cos_r, cos_r])
    space_sin = jnp.stack([sin_r, -sin_r])
    fields = propagate(
        fields,
        spec_cos,
        spec_sin,
        space_cos,
        space_sin,
        together_cols,
        together_rows,
        table_x,
        table_y,
    )
    values = fields.astype(jnp.float32)
    terms = [values[0, 0] * values[1, 0] + values[0, 1] * values[1, 1]]
    return (fields, jnp.stack(terms))


def per_device(flight_fields, top_fields, slowness, ref_slowness, flight_blocks, top_block):
    table_x = make_table(NX)
    table_y = make_table(NY)
    depth_idx = lax.axis_index("depth")
    first_block = flight_blocks[depth_idx]
    above_block = flight_blocks[jnp.maximum(depth_idx - 1, 0)]
    second_block = jnp.where(depth_idx == 0, top_block[0], above_block)
    after_first, first_terms = advance(
        flight_fields[0], first_block, slowness, ref_slowness, table_x, table_y
    )
    handed = passed_along(after_first, "depth", 1)
    incoming = jnp.where(depth_idx == 0, top_fields, handed)
    after_second, second_terms = advance(
        incoming, second_block, slowness, ref_slowness, table_x, table_y
    )
    return (first_terms + second_terms, after_second[None])


def solution(mesh):
    placed = (
        P("depth", None, None, "trans", None),
        P(None, None, "trans", None),
        P("depth", "trans", None),
        P("depth"),
        P(),
        P(),
    )
    return jax.shard_map(
        per_device,
        mesh=mesh,
        in_specs=placed,
        out_specs=(P("depth", "trans", None), P("depth", None, None, "trans", None)),
        check_vma=False,
    )
```

profile of v0, /device:TPU:7, one launch (start us, length us, event | category | flops | bytes accessed | tf_op | source)
XLA Modules:
  0.0 182.7 jit_solution(12908322561237548907)
XLA Ops:
  0.6 16.3 %fusion.29 = (f32[1024,1024]{1,0:T(8,128)S(1)}, f32[1024,1024]{1,0:T(8,128)S(1)}) fusion(), kind=kLoop, calls=%fused_computation.29 | loop fusion | flops 14680064 | bytes 8388608 | tf_op jit(solution)/shard_map/sin | solution.py:28
  17.0 1.1 fusion
  18.1 0.7 fusion.23
  18.8 1.2 copy-done.1
  20.1 0.8 copy.26
  20.9 1.7 reshape.547
  22.6 15.9 %all-to-all-start = ((bf16[32,2,2048]{2,1,0:T(2,128)(2,1)}), bf16[32,2,2048]{2,1,0:T(2,128)(2,1)S(1)}, u32[]{:S(2)}, u32[]{:S(2)}) async-start(bf16[32,2,2048]{2,1,0:T(2,128)(2,1)} %reshape.547), calls=%async_computation | async-start | bytes 524288 | tf_op jit(solution)/shard_map/all_to_all | solution.py:79
  39.2 0.7 fusion.124
  41.8 1.2 fusion.86
  43.0 17.5 %all-to-all-done = bf16[32,2,2048]{2,1,0:T(2,128)(2,1)S(1)} async-done(((bf16[32,2,2048]{2,1,0:T(2,128)(2,1)}), bf16[32,2,2048]{2,1,0:T(2,128)(2,1)S(1)}, u32[]{:S(2)}, u32[]{:S(2)}) %all-to-all-start) | async-done | bytes 262176 | tf_op jit(solution)/shard_map/all_to_all | solution.py:79
  60.5 0.5 reshape.548
  61.0 0.7 copy.65
  61.7 1.1 all_to_all.55
  62.8 3.0 %fusion.14 = f32[2,2,32,2048]{3,2,1,0:T(8,128)S(1)} fusion(bf16[2,2,32,1024]{3,2,1,0:T(8,128)(2,1)S(1)} %all_to_all.55, bf16[1024,2048]{1,0:T(8,128)(2,1)} %copy-done.1), kind=kOutput, calls=%fused_computation.18 | convolution fusion | flops 536870912 | bytes 5505024 | tf_op jit(solution)/shard_map/dot_general | solution.py:67
  66.0 0.2 copy-done.2
  66.3 0.7 fusion.12
  67.1 0.8 copy.28
  67.9 1.7 reshape.549
  69.6 4.5 %all-to-all-start.1 = ((bf16[32,2,2048]{2,1,0:T(2,128)(2,1)}), bf16[32,2,2048]{2,1,0:T(2,128)(2,1)S(1)}, u32[]{:S(2)}, u32[]{:S(2)}) async-start(bf16[32,2,2048]{2,1,0:T(2,128)(2,1)} %reshape.549), calls=%async_computation.1 | async-start | bytes 524288 | tf_op jit(solution)/shard_map/all_to_all | solution.py:83
  74.1 1.6 fusion.110
  75.7 20.4 %all-to-all-done.1 = bf16[32,2,2048]{2,1,0:T(2,128)(2,1)S(1)} async-done(((bf16[32,2,2048]{2,1,0:T(2,128)(2,1)}), bf16[32,2,2048]{2,1,0:T(2,128)(2,1)S(1)}, u32[]{:S(2)}, u32[]{:S(2)}) %all-to-all-start.1) | async-done | bytes 262176 | tf_op jit(solution)/shard_map/all_to_all | solution.py:83
  96.1 0.5 reshape.550
  96.6 0.7 copy.64
  97.3 1.1 all_to_all.59
  98.4 3.0 %fusion.18 = f32[2,2,32,2048]{3,2,0,1:T(8,128)S(1)} fusion(bf16[1024,2048]{1,0:T(8,128)(2,1)} %copy-done.1, bf16[2,2,1024,32]{2,3,1,0:T(8,128)(2,1)S(1)} %all_to_all.59), kind=kOutput, calls=%fused_computation.22 | convolution fusion | flops 536870912 | bytes 5505024 | tf_op jit(solution)/shard_map/fckr,ky->fcry/dot_general | solution.py:73
  101.5 0.1 fusion.59
  101.7 3.4 %collective-permute-start = (bf16[2,2,32,1024]{3,2,0,1:T(8,128)(2,1)S(1)}, bf16[2,2,32,1024]{3,2,0,1:T(8,128)(2,1)S(1)}, u32[]{:S(2)}, u32[]{:S(2)}) collective-permute-start(bf16[2,2,32,1024]{3,2,0,1:T(8,128)(2,1)S(1)} %get-tuple-element.23), channel_id=1, source_target_pairs={{0,32},{32,64},{64,96},{96,128},{128,160},{160,192},{192,224},{224... | collective-permute-start | bytes 786440 | tf_op jit(solution)/shard_map/ppermute | solution.py:20
  105.1 7.2 %collective-permute-done = bf16[2,2,32,1024]{3,2,0,1:T(8,128)(2,1)S(1)} collective-permute-done((bf16[2,2,32,1024]{3,2,0,1:T(8,128)(2,1)S(1)}, bf16[2,2,32,1024]{3,2,0,1:T(8,128)(2,1)S(1)}, u32[]{:S(2)}, u32[]{:S(2)}) %collective-permute-start) | collective-permute-done | bytes 262176 | tf_op jit(solution)/shard_map/ppermute | solution.py:20
  112.4 0.7 fusion.26
  113.2 0.8 copy.41
  114.0 1.0 reshape.551
  115.0 26.7 %all_to_all.72 = bf16[32,2,2048]{2,1,0:T(2,128)(2,1)S(1)} all-to-all(bf16[32,2,2048]{2,1,0:T(2,128)(2,1)S(1)} %reshape.551), channel_id=1, replica_groups=mesh['depth'=16,'trans'=32] {'trans'}, dimensions={0} | all-to-all | bytes 524288 | tf_op jit(solution)/shard_map/all_to_all | solution.py:79
  141.7 0.5 reshape.552
  142.2 0.7 copy.63
  142.9 1.1 all_to_all.63
  144.0 3.0 %fusion.8 = f32[2,2,32,2048]{3,2,1,0:T(8,128)S(1)} fusion(bf16[2,2,32,1024]{3,2,1,0:T(8,128)(2,1)S(1)} %all_to_all.63, bf16[1024,2048]{1,0:T(8,128)(2,1)} %copy-done.1), kind=kOutput, calls=%fused_computation.12 | convolution fusion | flops 536870912 | bytes 5505024 | tf_op jit(solution)/shard_map/dot_general | solution.py:67
  147.2 0.2 copy-done.4
  147.4 0.7 fusion.6
  148.3 0.8 copy.43
  149.0 1.0 reshape.553
  150.0 25.8 %all_to_all.73 = bf16[32,2,2048]{2,1,0:T(2,128)(2,1)S(1)} all-to-all(bf16[32,2,2048]{2,1,0:T(2,128)(2,1)S(1)} %reshape.553), channel_id=1, replica_groups=mesh['depth'=16,'trans'=32] {'trans'}, dimensions={0} | all-to-all | bytes 524288 | tf_op jit(solution)/shard_map/all_to_all | solution.py:83
  175.8 0.5 reshape.554
  176.3 0.7 copy.62
  177.0 1.1 all_to_all.67
  178.1 2.9 %fusion.4 = f32[2,2,32,2048]{3,2,1,0:T(8,128)S(1)} fusion(bf16[2,2,1024,32]{2,3,1,0:T(8,128)(2,1)S(1)} %all_to_all.67, bf16[1024,2048]{1,0:T(8,128)(2,1)} %copy-done.1), kind=kOutput, calls=%fused_computation.8 | convolution fusion | flops 536870912 | bytes 5505024 | tf_op jit(solution)/shard_map/fckr,ky->fcry/dot_general | solution.py:73
  181.0 0.1 fusion.75
  181.2 0.7 copy.47
  182.0 0.7 fusion.105
  (30 shorter events, 0.8 us)
Async XLA Ops:
  0.6 17.4 %copy-start = (bf16[1,2,2,32,1024]{4,3,2,1,0:T(8,128)(2,1)S(1)}, bf16[1,2,2,32,1024]{4,3,2,1,0:T(8,128)(2,1)}, u32[]{:S(2)}) copy-start(bf16[1,2,2,32,1024]{4,3,2,1,0:T(8,128)(2,1)} %param.6) | copy-start | bytes 786436
  18.1 2.0 %copy-start.1 = (bf16[1024,2048]{1,0:T(8,128)(2,1)}, bf16[1024,2048]{1,0:T(8,128)(2,1)S(1)}, u32[]{:S(2)}) copy-start(bf16[1024,2048]{1,0:T(8,128)(2,1)S(1)} %fusion) | copy-start | bytes 12582916
  20.0 19.2 %copy-start.7 = (s32[16]{0:T(128)S(1)}, s32[16]{0:T(128)}, u32[]{:S(2)}) copy-start(s32[16]{0:T(128)} %param.10) | copy-start | bytes 196
  22.6 37.9 %all-to-all-start = ((bf16[32,2,2048]{2,1,0:T(2,128)(2,1)}), bf16[32,2,2048]{2,1,0:T(2,128)(2,1)S(1)}, u32[]{:S(2)}, u32[]{:S(2)}) async-start(bf16[32,2,2048]{2,1,0:T(2,128)(2,1)} %reshape.547), calls=%async_computation | async-start | bytes 524288 | tf_op jit(solution)/shard_map/all_to_all | solution.py:79
  62.8 3.5 %copy-start.2 = (bf16[1024,2048]{1,0:T(8,128)(2,1)S(1)}, bf16[1024,2048]{1,0:T(8,128)(2,1)}, u32[]{:S(2)}) copy-start(bf16[1024,2048]{1,0:T(8,128)(2,1)} %copy-done.1) | copy-start | bytes 12582916
  66.3 7.8 %copy-start.6 = (f32[1,32,1024]{2,1,0:T(8,128)S(1)}, f32[1,32,1024]{2,1,0:T(8,128)}, u32[]{:S(2)}) copy-start(f32[1,32,1024]{2,1,0:T(8,128)} %param.8) | copy-start | bytes 393220
  69.6 26.5 %all-to-all-start.1 = ((bf16[32,2,2048]{2,1,0:T(2,128)(2,1)}), bf16[32,2,2048]{2,1,0:T(2,128)(2,1)S(1)}, u32[]{:S(2)}, u32[]{:S(2)}) async-start(bf16[32,2,2048]{2,1,0:T(2,128)(2,1)} %reshape.549), calls=%async_computation.1 | async-start | bytes 524288 | tf_op jit(solution)/shard_map/all_to_all | solution.py:83
  98.4 13.9 %copy-start.3 = (bf16[1024,2048]{1,0:T(8,128)(2,1)S(1)}, bf16[1024,2048]{1,0:T(8,128)(2,1)}, u32[]{:S(2)}) copy-start(bf16[1024,2048]{1,0:T(8,128)(2,1)} %copy-done.1) | copy-start | bytes 12582916
  98.4 13.9 %copy-start.8 = (bf16[2,2,32,1024]{3,2,1,0:T(8,128)(2,1)S(1)}, bf16[2,2,32,1024]{3,2,1,0:T(8,128)(2,1)}, u32[]{:S(2)}) copy-start(bf16[2,2,32,1024]{3,2,1,0:T(8,128)(2,1)} %param.7) | copy-start | bytes 786436
  101.7 10.7 %collective-permute-start = (bf16[2,2,32,1024]{3,2,0,1:T(8,128)(2,1)S(1)}, bf16[2,2,32,1024]{3,2,0,1:T(8,128)(2,1)S(1)}, u32[]{:S(2)}, u32[]{:S(2)}) collective-permute-start(bf16[2,2,32,1024]{3,2,0,1:T(8,128)(2,1)S(1)} %get-tuple-element.23), channel_id=1, source_target_pairs={{0,32},{32,64},{64,96},{96,128},{128,160},{160,192},{192,224},{224... | collective-permute-start | bytes 786440 | tf_op jit(solution)/shard_map/ppermute | solution.py:20
  144.0 3.5 %copy-start.4 = (bf16[1024,2048]{1,0:T(8,128)(2,1)S(1)}, bf16[1024,2048]{1,0:T(8,128)(2,1)}, u32[]{:S(2)}) copy-start(bf16[1024,2048]{1,0:T(8,128)(2,1)} %copy-done.1) | copy-start | bytes 12582916
  177.0 4.0 %copy-start.5 = (f32[1,1,32,1024]{3,2,1,0:T(8,128)S(1)}, f32[1,1,32,1024]{3,2,1,0:T(8,128)}, u32[]{:S(2)}) copy-start(f32[1,1,32,1024]{3,2,1,0:T(8,128)} %get-tuple-element.28) | copy-start | bytes 393220
where the time goes:
time: 184 us; the launch traced here: 183 us
  blocking collectives  52.5 us (29%)
  waiting for transfers between devices  45.1 us (25%)
  starting transfers between devices  23.9 us (13%)
  other arithmetic  22 us (12%)
  local copies, waits for them, and re-layouts  20.7 us (11%)
  matrix products  14.9 us (8%)
  between operations  3.65 us (2%)
    all_to_all x1, blocking collectives, together_cols(): lax.all_to_all(values, 'trans', split_axis=2, concat_axis=3, tiled=True)  26.7 us
    all_to_all x1, blocking collectives, together_rows(): lax.all_to_all(values, 'trans', split_axis=3, concat_axis=2, tiled=True)  25.8 us
    all_to_all x1, waiting for transfers between devices, together_rows(): lax.all_to_all(values, 'trans', split_axis=3, concat_axis=2, tiled=True)  20.4 us
    all_to_all x1, waiting for transfers between devices, together_cols(): lax.all_to_all(values, 'trans', split_axis=2, concat_axis=3, tiled=True)  17.5 us
    sin x1, other arithmetic, make_table(): jnp.sin(angles)  16.3 us
    all_to_all x1, starting transfers between devices, together_cols(): lax.all_to_all(values, 'trans', split_axis=2, concat_axis=3, tiled=True)  15.9 us
    unnamed x27, local copies, waits for them, and re-layouts  9.88 us
    ppermute x1, waiting for transfers between devices, passed_along(): lax.ppermute(value, axis, [(source, source + steps) for source in range(l...  7.22 us
  transfers between devices with their start and end apart: 3, of which 3 were waited for; matrix products, arithmetic and copies ran while one was open for 2% of the time, Pallas kernels for 0%

commit v1 on v0

v1 whole, which is shorter than its diff:
```python
import math

import jax
import jax.numpy as jnp
import ml_dtypes
import numpy as np
from jax import lax
from jax.experimental import pallas as pl
from jax.experimental.pallas import tpu as pltpu
from jax.sharding import PartitionSpec as P

MESH = pl.DeviceIdType.MESH
N = 1024
NFREQ = 256
DEPTH = 16
TRANS = 32
CHIPS = TRANS // 2
ROWS = N // TRANS
HALF = N // CHIPS
CHUNK = 256
omega_top = 4.0
step_length = 0.5


def make_table(length):
    positions = np.arange(length, dtype=np.int64)
    product = positions[:, None] * positions[None, :] % length
    angles = product.astype(np.float32) * np.float32(2.0 * math.pi / length)
    scaling = np.float32(1.0 / math.sqrt(length))
    table = np.concatenate([np.cos(angles), np.sin(angles)], axis=1) * scaling
    return table.astype(ml_dtypes.bfloat16)


def sine(x):
    y = x * x
    p = jnp.float32(1.0 / 355687428096000.0)
    for factorial in (1307674368000.0, 6227020800.0, 39916800.0, 362880.0, 5040.0, 120.0, 6.0, 1.0):
        p = 1.0 / factorial - y * p
    return x * p


def cosine(x):
    y = x * x
    p = jnp.float32(1.0 / 20922789888000.0)
    for factorial in (87178291200.0, 479001600.0, 3628800.0, 40320.0, 720.0, 24.0, 2.0, 1.0):
        p = 1.0 / factorial - y * p
    return p


def wavenumber(positions):
    signed = jnp.where(positions < N // 2, positions, positions - N)
    return signed.astype(jnp.float32) * (2.0 * math.pi / N)


def kernel(
    table_hbm, flight_hbm, top_hbm, slow_hbm, ref_s, flight_blocks, top_block,
    image, next_fields,
    table, flight, top, slow, first_image,
    d1, d3, e2, e4, handed,
    sa1, sa2, sa3, sa4, step1,
    lhs1, lhs2, rolled, shifted, back, spec_c, spec_s, rot_c, rot_s,
    load_sem, send_sem, recv_sem,
):
    s = lax.axis_index("depth")
    t = lax.axis_index("trans")
    chip, core = t // 2, lax.rem(t, 2)
    low = lax.broadcasted_iota(jnp.int32, (1, 128), 1) < 64
    plus = jnp.where(low, 1.0, -1.0)

    loads = [
        pltpu.make_async_copy(flight_hbm, flight, load_sem.at[0]),
        pltpu.make_async_copy(table_hbm, table, load_sem.at[1]),
        pltpu.make_async_copy(slow_hbm, slow, load_sem.at[2]),
        pltpu.make_async_copy(top_hbm, top, load_sem.at[3]),
    ]
    for load in loads:
        load.start()

    barrier = pltpu.get_barrier_semaphore()

    @pl.loop(1, TRANS)
    def _(i):
        pl.semaphore_signal(barrier, inc=1, device_id=(s, lax.rem(t + i, TRANS)), device_id_type=MESH)

    for shift in (1, DEPTH - 1):
        pl.semaphore_signal(barrier, inc=1, device_id=(lax.rem(s + shift, DEPTH), t), device_id_type=MESH)

    def remote(src, dst, sem_s, sem_r, dd, tt):
        pltpu.make_async_remote_copy(
            src_ref=src, dst_ref=dst, send_sem=send_sem.at[sem_s], recv_sem=recv_sem.at[sem_r],
            device_id=(dd, tt), device_id_type=MESH,
        ).start()

    def other_chip(j):
        m = (j + 1) // 2
        return lax.rem(chip + 8 + (1 - 2 * lax.rem(j, 2)) * m, CHIPS)

    def send_cols(f, src, dst, sem_s, sem_r):
        place = pl.ds(pl.multiple_of(t * ROWS, ROWS), ROWS)

        @pl.loop(0, CHIPS - 1)
        def _(j):
            q = other_chip(j)
            remote(src.at[q], dst.at[place], sem_s, sem_r, s, 2 * q + f)

        @pl.when(core == f)
        def _():
            pltpu.make_async_copy(src.at[chip], dst.at[place], recv_sem.at[sem_r]).start()

        @pl.when(core != f)
        def _():
            remote(src.at[chip], dst.at[place], sem_s, sem_r, s, 2 * chip + f)

    def sent_cols(f, src, sem_s):
        @pl.when(core == f)
        def _():
            part = src.at[pl.ds(0, CHIPS - 1)]
            pltpu.make_async_copy(part, part, send_sem.at[sem_s]).wait()

        @pl.when(core != f)
        def _():
            pltpu.make_async_copy(src, src, send_sem.at[sem_s]).wait()

    def send_rows(src, dst, sem_s, sem_r):
        @pl.loop(0, CHIPS - 1)
        def _(j):
            q = other_chip(j)
            for c in range(2):
                p = 2 * q + c
                rows = pl.ds(pl.multiple_of(p * ROWS, ROWS), ROWS)
                remote(src.at[rows], dst.at[core, chip], sem_s, sem_r + core, s, p)

        own = pl.ds(pl.multiple_of(t * ROWS, ROWS), ROWS)
        pltpu.make_async_copy(src.at[own], dst.at[core, chip], recv_sem.at[sem_r + core]).start()
        p = 2 * chip + 1 - core
        rows = pl.ds(pl.multiple_of(p * ROWS, ROWS), ROWS)
        remote(src.at[rows], dst.at[core, chip], sem_s, sem_r + core, s, p)

    def sent_rows(src, sem_s):
        part = src.at[pl.ds(0, N - ROWS)]
        pltpu.make_async_copy(part, part, send_sem.at[sem_s]).wait()

    def arrived(dst, sem_r):
        pltpu.make_async_copy(dst, dst, recv_sem.at[sem_r]).wait()

    def y_forward(src, dst):
        u = src[...]
        lhs1[...] = u
        lhs2[0:ROWS] = u[ROWS:]
        lhs2[ROWS:] = -u[:ROWS]

        @pl.loop(0, N // CHUNK)
        def _(j):
            start = pl.multiple_of(j * CHUNK, CHUNK)
            a = jnp.dot(lhs1[...], table[:, pl.ds(start, CHUNK)], preferred_element_type=jnp.float32)
            a += jnp.dot(lhs2[...], table[:, pl.ds(N + start, CHUNK)], preferred_element_type=jnp.float32)
            for h in range(CHUNK // 128):
                re = a[:ROWS, 128 * h : 128 * (h + 1)]
                im = a[ROWS:, 128 * h : 128 * (h + 1)]
                q = j * (CHUNK // 64) + 2 * h
                dst[q] = jnp.where(low, re, pltpu.roll(im, 64, 1)).astype(jnp.bfloat16)
                dst[q + 1] = jnp.where(low, pltpu.roll(re, 64, 1), im).astype(jnp.bfloat16)

    def x_stage(src, dst):
        @pl.loop(0, N // CHUNK)
        def _(i):
            rows = pl.ds(pl.multiple_of(i * CHUNK, CHUNK), CHUNK)
            d = src[rows].astype(jnp.float32)
            rolled[rows] = (pltpu.roll(d, 64, 1) * plus).astype(jnp.bfloat16)

        @pl.loop(0, N // CHUNK)
        def _(i):
            rows = pl.ds(pl.multiple_of(i * CHUNK, CHUNK), CHUNK)
            b = jnp.dot(table[rows, 0:N], src[...], preferred_element_type=jnp.float32)
            b += jnp.dot(table[rows, N : 2 * N], rolled[...], preferred_element_type=jnp.float32)
            b = b * spec_c[rows] + pltpu.roll(b, 64, 1) * spec_s[rows]
            shifted[rows] = b.astype(jnp.bfloat16)
            back[rows] = (pltpu.roll(b, 64, 1) * -plus).astype(jnp.bfloat16)

        @pl.loop(0, N // CHUNK)
        def _(i):
            rows = pl.ds(pl.multiple_of(i * CHUNK, CHUNK), CHUNK)
            c = jnp.dot(table[rows, 0:N], shifted[...], preferred_element_type=jnp.float32)
            c += jnp.dot(table[rows, N : 2 * N], back[...], preferred_element_type=jnp.float32)
            dst[rows] = c.astype(jnp.bfloat16)

    def y_inverse(src, f, finish):
        for j in range(CHIPS // 2):
            even = src[2 * j].astype(jnp.float32)
            odd = src[2 * j + 1].astype(jnp.float32)
            re = jnp.where(low, even, pltpu.roll(odd, 64, 1))
            im = jnp.where(low, pltpu.roll(even, 64, 1), odd)
            lanes = slice(128 * j, 128 * (j + 1))
            lhs1[0:ROWS, lanes] = re.astype(jnp.bfloat16)
            lhs1[ROWS:, lanes] = im.astype(jnp.bfloat16)
            lhs2[0:ROWS, lanes] = (-im).astype(jnp.bfloat16)
            lhs2[ROWS:, lanes] = re.astype(jnp.bfloat16)

        @pl.loop(0, N // CHUNK)
        def _(j):
            start = pl.multiple_of(j * CHUNK, CHUNK)
            v = jnp.dot(lhs1[...], table[:, pl.ds(start, CHUNK)], preferred_element_type=jnp.float32)
            v += jnp.dot(lhs2[...], table[:, pl.ds(N + start, CHUNK)], preferred_element_type=jnp.float32)
            finish(v, pl.ds(start, CHUNK))

    def stepped(v, cols, f):
        sign = 1.0 - 2.0 * f
        re, im = v[:ROWS], v[ROWS:]
        cosines, sines = rot_c[:, cols], rot_s[:, cols] * sign
        return (re * cosines - im * sines).astype(jnp.bfloat16), (re * sines + im * cosines).astype(jnp.bfloat16)

    def angles(block):
        angular = omega_top * (block.astype(jnp.float32) + 1.0) / NFREQ
        reference_s = ref_s[0]
        sign = jnp.where(core == 0, 1.0, -1.0)
        top_q = (angular * reference_s) * (angular * reference_s)
        lanes = lax.broadcasted_iota(jnp.int32, (1, 128), 1)
        wave_y = wavenumber(chip * HALF + lax.rem(lanes, 64))
        signs = -plus * sign

        @pl.loop(0, N // 64)
        def _(i):
            start = pl.multiple_of(i * 64, 64)
            wave_x = wavenumber(start + lax.broadcasted_iota(jnp.int32, (64, 1), 0))
            quad = top_q - wave_x * wave_x - wave_y * wave_y
            size = jnp.sqrt(jnp.abs(quad)) * step_length
            damping = jnp.where(quad < 0.0, jnp.exp(-size), 1.0)
            travel = jnp.where(quad < 0.0, 0.0, size)
            spec_c[pl.ds(start, 64)] = damping * cosine(travel)
            spec_s[pl.ds(start, 64)] = damping * sine(travel) * signs

        @pl.loop(0, N // CHUNK)
        def _(j):
            cols = pl.ds(pl.multiple_of(j * CHUNK, CHUNK), CHUNK)
            rotation = angular * (slow[:, cols] - reference_s) * step_length
            rot_c[:, cols] = cosine(rotation)
            rot_s[:, cols] = sine(rotation)

    loads[0].wait()
    loads[1].wait()
    y_forward(flight.at[0], sa1.at[0])
    pl.semaphore_wait(barrier, TRANS + 1)
    send_cols(0, sa1.at[0], d1, 0, 0)
    y_forward(flight.at[1], sa1.at[1])
    send_cols(1, sa1.at[1], d1, 1, 0)
    loads[2].wait()
    angles(flight_blocks[s])
    arrived(d1, 0)
    x_stage(d1, sa2)
    send_rows(sa2, e2, 2, 1)
    for f in range(2):
        arrived(e2.at[f], 1 + f)

        def finish_first(v, cols):
            re, im = stepped(v, cols, f)
            step1[f, :ROWS, cols] = re
            step1[f, ROWS:, cols] = im
            if f == 1:
                re, im = re.astype(jnp.float32), im.astype(jnp.float32)
                before = step1[0, :, cols].astype(jnp.float32)
                first_image[:, cols] = before[:ROWS] * re + before[ROWS:] * im

        y_inverse(e2.at[f], f, finish_first)

        @pl.when(s < DEPTH - 1)
        def _():
            remote(step1.at[f], handed.at[f], 3 + f, 3 + f, lax.rem(s + 1, DEPTH), t)

        if f == 0:
            loads[3].wait()

        @pl.when(s > 0)
        def _():
            arrived(handed.at[f], 3 + f)

        @pl.when(s == 0)
        def _():
            handed[f] = top[f]

        y_forward(handed.at[f], sa3.at[f])
        send_cols(f, sa3.at[f], d3, 5 + f, 5)

    above = flight_blocks[jnp.maximum(s - 1, 0)]
    angles(jnp.where(s == 0, top_block[0], above))
    arrived(d3, 5)
    x_stage(d3, sa4)
    send_rows(sa4, e4, 7, 6)
    for f in range(2):
        arrived(e4.at[f], 6 + f)

        def finish_second(v, cols):
            re, im = stepped(v, cols, f)
            next_fields[f, :ROWS, cols] = re
            next_fields[f, ROWS:, cols] = im
            if f == 1:
                re, im = re.astype(jnp.float32), im.astype(jnp.float32)
                before = next_fields[0, :, cols].astype(jnp.float32)
                image[:, cols] = first_image[:, cols] + (before[:ROWS] * re + before[ROWS:] * im)

        y_inverse(e4.at[f], f, finish_second)

    for f in range(2):
        sent_cols(f, sa1.at[f], f)
        sent_cols(f, sa3.at[f], 5 + f)

        @pl.when(s < DEPTH - 1)
        def _():
            pltpu.make_async_copy(step1.at[f], step1.at[f], send_sem.at[3 + f]).wait()

    sent_rows(sa2, 2)
    sent_rows(sa4, 7)


def per_device(flight_fields, top_fields, slowness, ref_slowness, flight_blocks, top_block):
    bf16, f32 = jnp.bfloat16, jnp.float32
    hbm = pl.BlockSpec(memory_space=pl.ANY)
    smem = pl.BlockSpec(memory_space=pltpu.SMEM)
    vmem = pl.BlockSpec(memory_space=pltpu.VMEM)
    pairs = (2, 2 * ROWS, N)
    planes = (CHIPS, ROWS, 128)
    image, after_second = pl.pallas_call(
        kernel,
        out_shape=(jax.ShapeDtypeStruct((ROWS, N), f32), jax.ShapeDtypeStruct(pairs, bf16)),
        in_specs=[hbm, hbm, hbm, hbm, smem, smem, smem],
        out_specs=(vmem, vmem),
        scratch_shapes=[
            pltpu.VMEM((N, 2 * N), bf16),
            pltpu.VMEM(pairs, bf16),
            pltpu.VMEM(pairs, bf16),
            pltpu.VMEM((ROWS, N), f32),
            pltpu.VMEM((ROWS, N), f32),
            pltpu.VMEM((N, 128), bf16),
            pltpu.VMEM((N, 128), bf16),
            pltpu.VMEM((2,) + planes, bf16),
            pltpu.VMEM((2,) + planes, bf16),
            pltpu.VMEM(pairs, bf16),
            pltpu.VMEM((2,) + planes, bf16),
            pltpu.VMEM((N, 128), bf16),
            pltpu.VMEM((2,) + planes, bf16),
            pltpu.VMEM((N, 128), bf16),
            pltpu.VMEM(pairs, bf16),
            pltpu.VMEM((2 * ROWS, N), bf16),
            pltpu.VMEM((2 * ROWS, N), bf16),
            pltpu.VMEM((N, 128), bf16),
            pltpu.VMEM((N, 128), bf16),
            pltpu.VMEM((N, 128), bf16),
            pltpu.VMEM((N, 128), f32),
            pltpu.VMEM((N, 128), f32),
            pltpu.VMEM((ROWS, N), f32),
            pltpu.VMEM((ROWS, N), f32),
            pltpu.SemaphoreType.DMA((4,)),
            pltpu.SemaphoreType.DMA((8,)),
            pltpu.SemaphoreType.DMA((8,)),
        ],
        compiler_params=pltpu.CompilerParams(collective_id=0, has_side_effects=True, vmem_limit_bytes=40 << 20),
        name="continuation",
    )(
        jnp.asarray(make_table(N)),
        flight_fields.reshape(pairs),
        top_fields.reshape(pairs),
        slowness.reshape(ROWS, N),
        ref_slowness,
        flight_blocks,
        top_block,
    )
    return image[None], after_second.reshape(1, 2, 2, ROWS, N)


def solution(mesh):
    placed = (
        P("depth", None, None, "trans", None),
        P(None, None, "trans", None),
        P("depth", "trans", None),
        P("depth"),
        P(),
        P(),
    )
    return jax.shard_map(
        per_device,
        mesh=mesh,
        in_specs=placed,
        out_specs=(P("depth", "trans", None), P("depth", None, None, "trans", None)),
        check_vma=False,
    )
```

time: 184 us -> 94 us (0.51)
  Pallas kernels: 0 us -> 84.4 us
  blocking collectives: 52.5 us -> 0 us
  waiting for transfers between devices: 45.1 us -> 0 us
  starting transfers between devices: 23.9 us -> 0 us
  other arithmetic: 22 us -> 0 us
  matrix products: 14.9 us -> 0 us
  local copies, waits for them, and re-layouts: 20.7 us -> 7 us
    pallas_call x0 -> x1, Pallas kernels: none -> 84.4 us  [per_device(): pl.pallas_call(kernel, out_shape=(jax.ShapeDtypeStruct((ROWS, N), f32), j...]
    all_to_all x2 -> x0, blocking collectives: 52.5 us -> none  [the longest x1 26.7 us: together_cols(): lax.all_to_all(values, 'trans', split_axis=2, concat_axis=3, tiled=True)]
    all_to_all x2 -> x0, waiting for transfers between devices: 37.9 us -> none  [the longest x1 20.4 us: together_rows(): lax.all_to_all(values, 'trans', split_axis=3, concat_axis=2, tiled=True)]
    all_to_all x2 -> x0, starting transfers between devices: 20.4 us -> none  [the longest x1 15.9 us: together_cols(): lax.all_to_all(values, 'trans', split_axis=2, concat_axis=3, tiled=True)]
    sin x1 -> x0, other arithmetic: 16.3 us -> none  [make_table(): jnp.sin(angles)]
    dot_general x8 -> x0, matrix products: 14.9 us -> none  [the longest x2 6.1 us: propagate(): product = jnp.dot(columns, table_x, preferred_element_type=jnp.float32)]
    ppermute x1 -> x0, waiting for transfers between devices: 7.22 us -> none  [passed_along(): lax.ppermute(value, axis, [(source, source + steps) for source in range(l...]
    all_to_all x8 -> x0, local copies, waits for them, and re-layouts: 7.08 us -> none  [the longest x4 3.54 us: together_rows(): lax.all_to_all(values, 'trans', split_axis=3, concat_axis=2, tiled=True)]
  transfers between devices with their start and end apart: 3 -> 0, of which waited for: 3 -> 0; matrix products, arithmetic and copies ran while one was open for 2% -> 0% of each run, Pallas kernels for 0% -> 0%
where the time goes in v1:
time: 94 us; the launch traced here: 93.3 us
  Pallas kernels  84.4 us (90%)
  local copies, waits for them, and re-layouts  7 us (7%)
  between operations  1.94 us (2%)
    pallas_call x1, Pallas kernels, per_device(): pl.pallas_call(kernel, out_shape=(jax.ShapeDtypeStruct((ROWS, N), f32), j...  84.4 us
    unnamed x12, local copies, waits for them, and re-layouts  7 us

profile of v1, /device:TPU:7, one launch (start us, length us, event | category | flops | bytes accessed | tf_op | source)
XLA Modules:
  0.0 93.3 jit_solution(9763614319228308017)
XLA Ops:
  1.9 0.0 copy-start
  1.9 2.2 %copy-done = bf16[1024,2048]{1,0:T(8,128)(2,1)S(1)} copy-done((bf16[1024,2048]{1,0:T(8,128)(2,1)S(1)}, bf16[1024,2048]{1,0:T(8,128)(2,1)}, u32[]{:S(2)}) %copy-start) | copy-done | bytes 4194328
  4.1 0.0 copy-start.1
  4.1 0.9 %copy-done.1 = bf16[1,2,2,32,1024]{4,3,2,1,0:T(8,128)(2,1)S(1)} copy-done((bf16[1,2,2,32,1024]{4,3,2,1,0:T(8,128)(2,1)S(1)}, bf16[1,2,2,32,1024]{4,3,2,1,0:T(8,128)(2,1)}, u32[]{:S(2)}) %copy-start.1) | copy-done | bytes 262168
  5.1 0.0 copy-start.2
  5.1 0.9 %copy-done.2 = bf16[2,2,32,1024]{3,2,1,0:T(8,128)(2,1)S(1)} copy-done((bf16[2,2,32,1024]{3,2,1,0:T(8,128)(2,1)S(1)}, bf16[2,2,32,1024]{3,2,1,0:T(8,128)(2,1)}, u32[]{:S(2)}) %copy-start.2) | copy-done | bytes 262168
  6.0 0.0 copy-start.3
  6.0 0.9 copy-done.3
  6.9 0.0 copy-start.4
  6.9 0.7 copy-done.4
  7.6 84.4 %continuation.1 = (f32[32,1024]{1,0:T(8,128)S(1)}, bf16[2,64,1024]{2,1,0:T(8,128)(2,1)S(1)}) custom-call(bf16[1024,2048]{1,0:T(8,128)(2,1)S(1)} %copy-done, bf16[2,64,1024]{2,1,0:T(8,128)(2,1)S(1)} %bitcast.5, bf16[2,64,1024]{2,1,0:T(8,128)(2,1)S(1)} %bitcast.6, f32[32,1024]{1,0:T(8,128)S(1)} %bitcast.8, f32[1]{0:T(128)S(6)} %copy.11.ref_s, ...), custom_call_target="tpu_custom_call" | custom-call | tf_op jit(solution)/shard_map/continuation/pallas_call | solution.py:321
  92.0 0.7 copy.13
  92.6 0.7 copy.14
Async XLA Ops:
  1.9 2.2 %copy-start = (bf16[1024,2048]{1,0:T(8,128)(2,1)S(1)}, bf16[1024,2048]{1,0:T(8,128)(2,1)}, u32[]{:S(2)}) copy-start(bf16[1024,2048]{1,0:T(8,128)(2,1)} %constant.2.clone.table_hbm) | copy-start | bytes 12582916
  4.1 0.9 %copy-start.1 = (bf16[1,2,2,32,1024]{4,3,2,1,0:T(8,128)(2,1)S(1)}, bf16[1,2,2,32,1024]{4,3,2,1,0:T(8,128)(2,1)}, u32[]{:S(2)}) copy-start(bf16[1,2,2,32,1024]{4,3,2,1,0:T(8,128)(2,1)} %param.7) | copy-start | bytes 786436
  5.1 0.9 %copy-start.2 = (bf16[2,2,32,1024]{3,2,1,0:T(8,128)(2,1)S(1)}, bf16[2,2,32,1024]{3,2,1,0:T(8,128)(2,1)}, u32[]{:S(2)}) copy-start(bf16[2,2,32,1024]{3,2,1,0:T(8,128)(2,1)} %param.8) | copy-start | bytes 786436
  6.0 0.9 copy-start.3
  6.9 0.7 copy-start.4

commit v2 on v1

v2 whole, which is shorter than its diff:
```python
import math

import jax
import jax.numpy as jnp
import ml_dtypes
import numpy as np
from jax import lax
from jax.experimental import pallas as pl
from jax.experimental.pallas import tpu as pltpu
from jax.sharding import PartitionSpec as P

MESH = pl.DeviceIdType.MESH
N = 1024
NFREQ = 256
DEPTH = 16
TRANS = 32
CHIPS = TRANS // 2
ROWS = N // TRANS
HALF = N // CHIPS
Q = N // 4
BLOCK = 64
omega_top = 4.0
step_length = 0.5
f32 = jnp.float32
bf16 = jnp.bfloat16


def make_tables():
    k = 4 * np.arange(Q)[None, :, None] + np.arange(4)[:, None, None]
    angles = (k * np.arange(Q)[None, None, :] % N) * (2.0 * math.pi / N)
    parts = np.stack([np.cos(angles), np.sin(angles)], axis=1) / math.sqrt(N)
    stacked = parts.reshape(4, 2 * Q, Q)
    flipped = parts.transpose(0, 1, 3, 2).reshape(4, 2 * Q, Q)
    return stacked.astype(ml_dtypes.bfloat16), flipped.astype(ml_dtypes.bfloat16)


def sine(x):
    y = x * x
    p = 1.0 / 355687428096000.0
    for factorial in (1307674368000.0, 6227020800.0, 39916800.0, 362880.0, 5040.0, 120.0, 6.0, 1.0):
        p = 1.0 / factorial - y * p
    return x * p


def cosine(x):
    y = x * x
    p = 1.0 / 20922789888000.0
    for factorial in (87178291200.0, 479001600.0, 3628800.0, 40320.0, 720.0, 24.0, 2.0, 1.0):
        p = 1.0 / factorial - y * p
    return p


def wavenumber(positions):
    signed = jnp.where(positions < N // 2, positions, positions - N)
    return signed.astype(f32) * (2.0 * math.pi / N)


def low_lanes():
    return lax.broadcasted_iota(jnp.int32, (1, 128), 1) < 64


def times_i(v):
    return pltpu.roll(v, 64, 1) * jnp.where(low_lanes(), -1.0, 1.0)


def turned(v):
    return jnp.concatenate([-v[ROWS:], v[:ROWS]], axis=0)


def y_forward(u, tables, dst):
    low = low_lanes()
    u0, u1, u2, u3 = (u[:, Q * j : Q * (j + 1)].astype(f32) for j in range(4))
    a, b, c, d = u0 + u2, u1 + u3, u0 - u2, turned(u1 - u3)
    for r, v in enumerate((a + b, c - d, a - b, c + d)):
        v = v.astype(bf16)
        left = jnp.concatenate([v, -turned(v)], axis=1)
        out = jnp.dot(left, tables[r], preferred_element_type=f32)
        for h in range(2):
            re = out[:ROWS, 128 * h : 128 * (h + 1)]
            im = out[ROWS:, 128 * h : 128 * (h + 1)]
            q = 4 * r + 2 * h
            dst[q] = jnp.where(low, re, pltpu.roll(im, 64, 1)).astype(bf16)
            dst[q + 1] = jnp.where(low, pltpu.roll(re, 64, 1), im).astype(bf16)


def y_inverse(src, tables):
    low = low_lanes()
    w = []
    for r in range(4):
        re, im = [], []
        for h in range(2):
            even = src[4 * r + 2 * h].astype(f32)
            odd = src[4 * r + 2 * h + 1].astype(f32)
            re.append(jnp.where(low, even, pltpu.roll(odd, 64, 1)))
            im.append(jnp.where(low, pltpu.roll(even, 64, 1), odd))
        v = jnp.concatenate([jnp.concatenate(re, axis=1), jnp.concatenate(im, axis=1)], axis=0).astype(bf16)
        left = jnp.concatenate([v, turned(v)], axis=1)
        w.append(jnp.dot(left, tables[r], preferred_element_type=f32))
    a, b, c, d = w[0] + w[2], w[1] + w[3], w[0] - w[2], turned(w[1] - w[3])
    return a + b, c + d, a - b, c - d


def x_stage(src, dst, tables, flipped, spec_c, spec_s, v_ref, g_ref, w_ref):
    for i in range(Q // BLOCK):
        rows = slice(BLOCK * i, BLOCK * (i + 1))
        u0, u1, u2, u3 = (src[Q * j + BLOCK * i : Q * j + BLOCK * (i + 1)].astype(f32) for j in range(4))
        a, b, c, d = u0 + u2, u1 + u3, u0 - u2, times_i(u1 - u3)
        for r, v in enumerate((a + b, c - d, a - b, c + d)):
            v_ref[r, rows] = v.astype(bf16)
    for r in range(4):
        out = jnp.dot(tables[r], v_ref[r], preferred_element_type=f32)
        p, q = out[:Q], out[Q:]
        cosines, sines = spec_c[Q * r : Q * (r + 1)], spec_s[Q * r : Q * (r + 1)]
        g_ref[r] = (p * cosines + q * sines + times_i(p * sines - q * cosines)).astype(bf16)
    for r in range(4):
        w_ref[r] = jnp.dot(flipped[r], g_ref[r], preferred_element_type=f32)
    for i in range(Q // BLOCK):
        p = [w_ref[r, BLOCK * i : BLOCK * (i + 1)] for r in range(4)]
        q = [w_ref[r, Q + BLOCK * i : Q + BLOCK * (i + 1)] for r in range(4)]
        pa, pb, pc, pd = p[0] + p[2], p[1] + p[3], p[0] - p[2], p[1] - p[3]
        qa, qb, qc, qd = q[0] + q[2], q[1] + q[3], q[0] - q[2], q[1] - q[3]
        pairs = ((pa + pb, qa + qb), (pc - qd, qc + pd), (pa - pb, qa - qb), (pc + qd, qc - pd))
        for j, (re, im) in enumerate(pairs):
            dst[Q * j + BLOCK * i : Q * j + BLOCK * (i + 1)] = (re + times_i(im)).astype(bf16)


def spectral(angular, reference_s, chip, sign, spec_c, spec_s):
    square = (angular * reference_s) * (angular * reference_s)
    lanes = lax.broadcasted_iota(jnp.int32, (1, 128), 1)
    wave_y = wavenumber(4 * (HALF * lax.rem(chip, 4) + lax.rem(lanes, 64)) + chip // 4)

    @pl.loop(0, N // BLOCK)
    def _(i):
        start = pl.multiple_of(i * BLOCK, BLOCK)
        r, first = i // (Q // BLOCK), lax.rem(i, Q // BLOCK) * BLOCK
        wave_x = wavenumber(4 * (first + lax.broadcasted_iota(jnp.int32, (BLOCK, 1), 0)) + r)
        quad = square - wave_x * wave_x - wave_y * wave_y
        size = jnp.sqrt(jnp.abs(quad)) * step_length
        damping = jnp.where(quad < 0.0, jnp.exp(-size), 1.0)
        travel = jnp.where(quad < 0.0, 0.0, size)
        spec_c[pl.ds(start, BLOCK)] = damping * cosine(travel)
        spec_s[pl.ds(start, BLOCK)] = damping * sine(travel) * sign


def rotations(angular, reference_s, slow, rot_c, rot_s):
    @pl.loop(0, 4)
    def _(j):
        cols = pl.ds(pl.multiple_of(j * Q, Q), Q)
        rotation = angular * (slow[:, cols] - reference_s) * step_length
        rot_c[:, cols] = cosine(rotation)
        rot_s[:, cols] = sine(rotation)


def rotated(v, cosines, sines):
    re, im = v[:ROWS], v[ROWS:]
    return jnp.concatenate([re * cosines - im * sines, re * sines + im * cosines], axis=0).astype(bf16)


def correlation(source, receiver):
    source, receiver = source.astype(f32), receiver.astype(f32)
    return source[:ROWS] * receiver[:ROWS] + source[ROWS:] * receiver[ROWS:]


def kernel(
    tables_hbm, flipped_hbm, flight_hbm, top_hbm, slow_hbm, ref_s, flight_blocks, top_block,
    image, next_fields,
    tables, flipped, flight, top, slow, first_image,
    d1, d3, e2, e4, sa1, sa2, sa3, sa4, step1,
    v_ref, g_ref, w_ref, spec_c, spec_s, rot_c, rot_s,
    load_sem, send_sem, recv_sem,
):
    s = lax.axis_index("depth")
    t = lax.axis_index("trans")
    chip, core = t // 2, lax.rem(t, 2)
    below, above = lax.rem(s + 1, DEPTH), lax.rem(s + DEPTH - 1, DEPTH)

    barrier = pltpu.get_barrier_semaphore()

    @pl.loop(1, TRANS)
    def _(i):
        pl.semaphore_signal(barrier, inc=1, device_id=(s, lax.rem(t + i, TRANS)), device_id_type=MESH)

    @pl.loop(0, TRANS)
    def _(i):
        pl.semaphore_signal(barrier, inc=1, device_id=(below, i), device_id_type=MESH)
        pl.semaphore_signal(barrier, inc=1, device_id=(above, i), device_id_type=MESH)

    loads = [
        pltpu.make_async_copy(src, dst, load_sem.at[i])
        for i, (src, dst) in enumerate(
            ((flight_hbm, flight), (flipped_hbm, flipped), (slow_hbm, slow), (tables_hbm, tables), (top_hbm, top))
        )
    ]
    for load in loads:
        load.start()

    def remote(src, dst, sem_s, sem_r, dd, tt):
        pltpu.make_async_remote_copy(
            src_ref=src, dst_ref=dst, send_sem=send_sem.at[sem_s], recv_sem=recv_sem.at[sem_r],
            device_id=(dd, tt), device_id_type=MESH,
        ).start()

    def other_chip(j):
        m = (j + 1) // 2
        return lax.rem(chip + 8 + (1 - 2 * lax.rem(j, 2)) * m, CHIPS)

    place = pl.ds(pl.multiple_of(t * ROWS, ROWS), ROWS)

    def send_cols(f, src, dst, sem_s, sem_r):
        @pl.loop(0, CHIPS - 1)
        def _(j):
            q = other_chip(j)
            remote(src.at[q], dst.at[place], sem_s, sem_r, s, 2 * q + f)

        @pl.when(core == f)
        def _():
            pltpu.make_async_copy(src.at[chip], dst.at[place], recv_sem.at[sem_r]).start()

        @pl.when(core != f)
        def _():
            remote(src.at[chip], dst.at[place], sem_s, sem_r, s, 2 * chip + f)

    def sent_cols(f, src, sem_s):
        @pl.when(core == f)
        def _():
            part = src.at[pl.ds(0, CHIPS - 1)]
            pltpu.make_async_copy(part, part, send_sem.at[sem_s]).wait()

        @pl.when(core != f)
        def _():
            sent(src, sem_s)

    def send_below(f, src, dst, sem_s, sem_r):
        @pl.loop(0, CHIPS)
        def _(j):
            q = other_chip(j)
            remote(src.at[q], dst.at[place], sem_s, sem_r, below, 2 * q + f)

    def send_rows(src, dst, sem_s, sem_r):
        @pl.loop(0, CHIPS - 1)
        def _(j):
            q = other_chip(j)
            for c in range(2):
                p = 2 * q + c
                rows = pl.ds(pl.multiple_of(p * ROWS, ROWS), ROWS)
                remote(src.at[rows], dst.at[core, chip], sem_s, sem_r + core, s, p)

        pltpu.make_async_copy(src.at[place], dst.at[core, chip], recv_sem.at[sem_r + core]).start()
        p = 2 * chip + 1 - core
        rows = pl.ds(pl.multiple_of(p * ROWS, ROWS), ROWS)
        remote(src.at[rows], dst.at[core, chip], sem_s, sem_r + core, s, p)

    def sent(src, sem_s):
        pltpu.make_async_copy(src, src, send_sem.at[sem_s]).wait()

    def arrived(dst, sem_r):
        pltpu.make_async_copy(dst, dst, recv_sem.at[sem_r]).wait()

    loads[0].wait()
    loads[1].wait()
    y_forward(flight[0], flipped, sa1.at[0])
    pl.semaphore_wait(barrier, 3 * TRANS - 1)
    send_cols(0, sa1.at[0], d1, 0, 0)
    y_forward(flight[1], flipped, sa1.at[1])
    send_cols(1, sa1.at[1], d1, 1, 0)
    for load in loads[2:]:
        load.wait()
    reference_s = ref_s[0]
    sign = jnp.where(core == 0, 1.0, -1.0)
    first = flight_blocks[s]
    second = jnp.where(s == 0, top_block[0], flight_blocks[jnp.maximum(s - 1, 0)])
    for step, block in enumerate((first, second)):
        angular = omega_top * (block.astype(f32) + 1.0) / NFREQ
        spectral(angular, reference_s, chip, sign, spec_c.at[step], spec_s.at[step])
        rotations(angular, reference_s, slow, rot_c.at[step], rot_s.at[step])
    arrived(d1, 0)
    x_stage(d1, sa2, tables, flipped, spec_c.at[0], spec_s.at[0], v_ref, g_ref, w_ref)
    send_rows(sa2, e2, 2, 1)
    for f in range(2):
        arrived(e2.at[f], 1 + f)
        for j, v in enumerate(y_inverse(e2.at[f], tables)):
            cols = slice(Q * j, Q * (j + 1))
            now = rotated(v, rot_c[0, :, cols], rot_s[0, :, cols] * (1.0 - 2.0 * f))
            if f == 0:
                step1[0, :, cols] = now
            else:
                first_image[:, cols] = correlation(step1[0, :, cols], now)
            step1[1, :, cols] = jnp.where(s == DEPTH - 1, top[f, :, cols], now)
        y_forward(step1[1], flipped, sa3.at[f])
        send_below(f, sa3.at[f], d3, 3 + f, 3)

    arrived(d3, 3)
    x_stage(d3, sa4, tables, flipped, spec_c.at[1], spec_s.at[1], v_ref, g_ref, w_ref)
    send_rows(sa4, e4, 5, 4)
    for f in range(2):
        arrived(e4.at[f], 4 + f)
        for j, v in enumerate(y_inverse(e4.at[f], tables)):
            cols = slice(Q * j, Q * (j + 1))
            now = rotated(v, rot_c[1, :, cols], rot_s[1, :, cols] * (1.0 - 2.0 * f))
            next_fields[f, :, cols] = now
            if f == 1:
                image[:, cols] = first_image[:, cols] + correlation(next_fields[0, :, cols], now)

    for f in range(2):
        sent_cols(f, sa1.at[f], f)
        sent(sa3.at[f], 3 + f)
    for src, sem in ((sa2, 2), (sa4, 5)):
        sent(src.at[pl.ds(0, N - ROWS)], sem)


def per_device(flight_fields, top_fields, slowness, ref_slowness, flight_blocks, top_block):
    hbm = pl.BlockSpec(memory_space=pltpu.HBM)
    smem = pl.BlockSpec(memory_space=pltpu.SMEM)
    vmem = pl.BlockSpec(memory_space=pltpu.VMEM)
    pairs = (2, 2 * ROWS, N)
    planes = (2, CHIPS, ROWS, 128)
    stacked, flipped = make_tables()
    image, after_second = pl.pallas_call(
        kernel,
        out_shape=(jax.ShapeDtypeStruct((ROWS, N), f32), jax.ShapeDtypeStruct(pairs, bf16)),
        in_specs=[hbm] * 5 + [smem] * 3,
        out_specs=(vmem, vmem),
        scratch_shapes=[
            pltpu.VMEM((4, 2 * Q, Q), bf16),
            pltpu.VMEM((4, 2 * Q, Q), bf16),
            pltpu.VMEM(pairs, bf16),
            pltpu.VMEM(pairs, bf16),
            pltpu.VMEM((ROWS, N), f32),
            pltpu.VMEM((ROWS, N), f32),
            pltpu.VMEM((N, 128), bf16),
            pltpu.VMEM((N, 128), bf16),
            pltpu.VMEM(planes, bf16),
            pltpu.VMEM(planes, bf16),
            pltpu.VMEM(planes, bf16),
            pltpu.VMEM((N, 128), bf16),
            pltpu.VMEM(planes, bf16),
            pltpu.VMEM((N, 128), bf16),
            pltpu.VMEM(pairs, bf16),
            pltpu.VMEM((4, Q, 128), bf16),
            pltpu.VMEM((4, Q, 128), bf16),
            pltpu.VMEM((4, 2 * Q, 128), f32),
            pltpu.VMEM((2, N, 128), f32),
            pltpu.VMEM((2, N, 128), f32),
            pltpu.VMEM((2, ROWS, N), f32),
            pltpu.VMEM((2, ROWS, N), f32),
            pltpu.SemaphoreType.DMA((5,)),
            pltpu.SemaphoreType.DMA((6,)),
            pltpu.SemaphoreType.DMA((6,)),
        ],
        compiler_params=pltpu.CompilerParams(collective_id=0, has_side_effects=True, vmem_limit_bytes=60 << 20),
        name="continuation",
    )(
        jnp.asarray(stacked),
        jnp.asarray(flipped),
        flight_fields.reshape(pairs),
        top_fields.reshape(pairs),
        slowness.reshape(ROWS, N),
        ref_slowness,
        flight_blocks,
        top_block,
    )
    return image[None], after_second.reshape(1, 2, 2, ROWS, N)


def solution(mesh):
    placed = (
        P("depth", None, None, "trans", None),
        P(None, None, "trans", None),
        P("depth", "trans", None),
        P("depth"),
        P(),
        P(),
    )
    return jax.shard_map(
        per_device,
        mesh=mesh,
        in_specs=placed,
        out_specs=(P("depth", "trans", None), P("depth", None, None, "trans", None)),
        check_vma=False,
    )
```

time: 94 us -> 77.1 us (0.82)
  the two profiles are of different devices: /device:TPU:7 before, /device:TPU:1 now
where the time goes in v2:
time: 77.1 us; the launch traced here: 76.9 us
  Pallas kernels  72.7 us (94%)
  local copies, waits for them, and re-layouts  2.32 us (3%)
  between operations  1.94 us (3%)
    pallas_call x1, Pallas kernels, per_device(): pl.pallas_call(kernel, out_shape=(jax.ShapeDtypeStruct((ROWS, N), f32), j...  72.7 us
    unnamed x4, local copies, waits for them, and re-layouts  2.32 us

profile of v2, /device:TPU:1, one launch (start us, length us, event | category | flops | bytes accessed | tf_op | source)
XLA Modules:
  0.0 76.9 jit_solution(17842966901474608346)
XLA Ops:
  1.9 72.7 %continuation.1 = (f32[32,1024]{1,0:T(8,128)}, bf16[2,64,1024]{2,1,0:T(8,128)(2,1)}) custom-call(bf16[4,512,256]{2,1,0:T(8,128)(2,1)} %constant.4.clone.tables_hbm, bf16[4,512,256]{2,1,0:T(8,128)(2,1)} %constant.5.clone.flipped_hbm, bf16[2,64,1024]{2,1,0:T(8,128)(2,1)} %bitcast.6, bf16[2,64,1024]{2,1,0:T(8,128)(2,1)} %bitcast.7, f32[32,1024]{1,0:T(8,128)} %bitcast.8, ...), custom_call_target="tpu_custom_call" | custom-call | tf_op jit(solution)/shard_map/continuation/pallas_call | solution.py:318
  74.6 0.0 copy-start
  74.6 1.6 %copy.14 = f32[1,32,1024]{2,1,0:T(8,128)} copy(f32[1,32,1024]{2,1,0:T(8,128)} %bitcast.9) | data formatting | bytes 262144
  76.2 0.0 copy-done
  76.2 0.7 copy.15
Async XLA Ops:
  74.6 1.6 %copy-start = (bf16[2,64,1024]{2,1,0:T(8,128)(2,1)S(1)}, bf16[2,64,1024]{2,1,0:T(8,128)(2,1)}, u32[]{:S(2)}) copy-start(bf16[2,64,1024]{2,1,0:T(8,128)(2,1)} %get-tuple-element.5) | copy-start | bytes 786436

commit v3 on v2

--- a/solution.py
+++ b/solution.py
@@ -167,23 +167,12 @@
     tables, flipped, flight, top, slow, first_image,
     d1, d3, e2, e4, sa1, sa2, sa3, sa4, step1,
     v_ref, g_ref, w_ref, spec_c, spec_s, rot_c, rot_s,
-    load_sem, send_sem, recv_sem,
+    load_sem, send_sem, recv_sem, entered,
 ):
     s = lax.axis_index("depth")
     t = lax.axis_index("trans")
     chip, core = t // 2, lax.rem(t, 2)
     below, above = lax.rem(s + 1, DEPTH), lax.rem(s + DEPTH - 1, DEPTH)
-
-    barrier = pltpu.get_barrier_semaphore()
-
-    @pl.loop(1, TRANS)
-    def _(i):
-        pl.semaphore_signal(barrier, inc=1, device_id=(s, lax.rem(t + i, TRANS)), device_id_type=MESH)
-
-    @pl.loop(0, TRANS)
-    def _(i):
-        pl.semaphore_signal(barrier, inc=1, device_id=(below, i), device_id_type=MESH)
-        pl.semaphore_signal(barrier, inc=1, device_id=(above, i), device_id_type=MESH)
 
     loads = [
         pltpu.make_async_copy(src, dst, load_sem.at[i])
@@ -191,7 +180,19 @@
             ((flight_hbm, flight), (flipped_hbm, flipped), (slow_hbm, slow), (tables_hbm, tables), (top_hbm, top))
         )
     ]
-    for load in loads:
+    for load in loads[:2]:
+        load.start()
+
+    barrier = pltpu.get_barrier_semaphore()
+
+    @pl.loop(1, TRANS)
+    def _(i):
+        pl.semaphore_signal(barrier, inc=1, device_id=(s, lax.rem(t + i, TRANS)), device_id_type=MESH)
+
+    for neighbour in (below, above):
+        pl.semaphore_signal(barrier, inc=1, device_id=(neighbour, t), device_id_type=MESH)
+
+    for load in loads[2:]:
         load.start()
 
     def remote(src, dst, sem_s, sem_r, dd, tt):
@@ -259,7 +260,8 @@
     loads[0].wait()
     loads[1].wait()
     y_forward(flight[0], flipped, sa1.at[0])
-    pl.semaphore_wait(barrier, 3 * TRANS - 1)
+    pl.semaphore_wait(barrier, TRANS + 1)
+    pl.semaphore_signal(entered, inc=1, device_id=(above, t), device_id_type=MESH)
     send_cols(0, sa1.at[0], d1, 0, 0)
     y_forward(flight[1], flipped, sa1.at[1])
     send_cols(1, sa1.at[1], d1, 1, 0)
@@ -287,6 +289,8 @@
                 first_image[:, cols] = correlation(step1[0, :, cols], now)
             step1[1, :, cols] = jnp.where(s == DEPTH - 1, top[f, :, cols], now)
         y_forward(step1[1], flipped, sa3.at[f])
+        if f == 0:
+            pl.semaphore_wait(entered, 1)
         send_below(f, sa3.at[f], d3, 3 + f, 3)
 
     arrived(d3, 3)
@@ -346,6 +350,7 @@
             pltpu.SemaphoreType.DMA((5,)),
             pltpu.SemaphoreType.DMA((6,)),
             pltpu.SemaphoreType.DMA((6,)),
+            pltpu.SemaphoreType.REGULAR,
         ],
         compiler_params=pltpu.CompilerParams(collective_id=0, has_side_effects=True, vmem_limit_bytes=60 << 20),
         name="continuation",

time: 77.1 us -> 77.1 us (level)
  no operation moved by 1% of the time
where the time goes in v3:
time: 77.1 us; the launch traced here: 76.9 us
  Pallas kernels  72.6 us (94%)
  local copies, waits for them, and re-layouts  2.32 us (3%)
  between operations  1.94 us (3%)
    pallas_call x1, Pallas kernels, per_device(): pl.pallas_call(kernel, out_shape=(jax.ShapeDtypeStruct((ROWS, N), f32), j...  72.6 us
    unnamed x4, local copies, waits for them, and re-layouts  2.32 us

profile of v3, /device:TPU:1, one launch (start us, length us, event | category | flops | bytes accessed | tf_op | source)
XLA Modules:
  0.0 76.9 jit_solution(18386541117275461321)
XLA Ops:
  1.9 72.6 %continuation.1 = (f32[32,1024]{1,0:T(8,128)}, bf16[2,64,1024]{2,1,0:T(8,128)(2,1)}) custom-call(bf16[4,512,256]{2,1,0:T(8,128)(2,1)} %constant.4.clone.tables_hbm, bf16[4,512,256]{2,1,0:T(8,128)(2,1)} %constant.5.clone.flipped_hbm, bf16[2,64,1024]{2,1,0:T(8,128)(2,1)} %bitcast.6, bf16[2,64,1024]{2,1,0:T(8,128)(2,1)} %bitcast.7, f32[32,1024]{1,0:T(8,128)} %bitcast.8, ...), custom_call_target="tpu_custom_call" | custom-call | tf_op jit(solution)/shard_map/continuation/pallas_call | solution.py:322
  74.6 0.0 copy-start
  74.6 1.6 %copy.14 = f32[1,32,1024]{2,1,0:T(8,128)} copy(f32[1,32,1024]{2,1,0:T(8,128)} %bitcast.9) | data formatting | bytes 262144
  76.2 0.0 copy-done
  76.2 0.7 copy.15
Async XLA Ops:
  74.6 1.6 %copy-start = (bf16[2,64,1024]{2,1,0:T(8,128)(2,1)S(1)}, bf16[2,64,1024]{2,1,0:T(8,128)(2,1)}, u32[]{:S(2)}) copy-start(bf16[2,64,1024]{2,1,0:T(8,128)(2,1)} %get-tuple-element.5) | copy-start | bytes 786436

commit v4 on v3

--- a/solution.py
+++ b/solution.py
@@ -162,12 +162,12 @@
 
 
 def kernel(
-    tables_hbm, flipped_hbm, flight_hbm, top_hbm, slow_hbm, ref_s, flight_blocks, top_block,
+    tables_hbm, flipped_hbm, flight_hbm, top_hbm, slow_hbm, scalars_hbm,
     image, next_fields,
     tables, flipped, flight, top, slow, first_image,
     d1, d3, e2, e4, sa1, sa2, sa3, sa4, step1,
     v_ref, g_ref, w_ref, spec_c, spec_s, rot_c, rot_s,
-    load_sem, send_sem, recv_sem, entered,
+    scalars, load_sem, send_sem, recv_sem, entered,
 ):
     s = lax.axis_index("depth")
     t = lax.axis_index("trans")
@@ -177,7 +177,7 @@
     loads = [
         pltpu.make_async_copy(src, dst, load_sem.at[i])
         for i, (src, dst) in enumerate(
-            ((flight_hbm, flight), (flipped_hbm, flipped), (slow_hbm, slow), (tables_hbm, tables), (top_hbm, top))
+            ((flight_hbm, flight), (flipped_hbm, flipped), (slow_hbm, slow), (tables_hbm, tables), (top_hbm, top), (scalars_hbm, scalars))
         )
     ]
     for load in loads[:2]:
@@ -267,12 +267,20 @@
     send_cols(1, sa1.at[1], d1, 1, 0)
     for load in loads[2:]:
         load.wait()
-    reference_s = ref_s[0]
+    pl.semaphore_wait(entered, 1)
+
+    @pl.when(s == DEPTH - 1)
+    def _():
+        for f in range(2):
+            y_forward(top[f], flipped, sa3.at[f])
+            send_below(f, sa3.at[f], d3, 3 + f, 3)
+
+    reference_s = scalars[DEPTH + 1]
     sign = jnp.where(core == 0, 1.0, -1.0)
-    first = flight_blocks[s]
-    second = jnp.where(s == 0, top_block[0], flight_blocks[jnp.maximum(s - 1, 0)])
+    first = scalars[s]
+    second = jnp.where(s == 0, scalars[DEPTH], scalars[jnp.maximum(s - 1, 0)])
     for step, block in enumerate((first, second)):
-        angular = omega_top * (block.astype(f32) + 1.0) / NFREQ
+        angular = omega_top * (block + 1.0) / NFREQ
         spectral(angular, reference_s, chip, sign, spec_c.at[step], spec_s.at[step])
         rotations(angular, reference_s, slow, rot_c.at[step], rot_s.at[step])
     arrived(d1, 0)
@@ -283,15 +291,15 @@
         for j, v in enumerate(y_inverse(e2.at[f], tables)):
             cols = slice(Q * j, Q * (j + 1))
             now = rotated(v, rot_c[0, :, cols], rot_s[0, :, cols] * (1.0 - 2.0 * f))
-            if f == 0:
-                step1[0, :, cols] = now
-            else:
+            step1[f, :, cols] = now
+            if f == 1:
                 first_image[:, cols] = correlation(step1[0, :, cols], now)
-            step1[1, :, cols] = jnp.where(s == DEPTH - 1, top[f, :, cols], now)
-        y_forward(step1[1], flipped, sa3.at[f])
-        if f == 0:
-            pl.semaphore_wait(entered, 1)
-        send_below(f, sa3.at[f], d3, 3 + f, 3)
+
+        @pl.when(s < DEPTH - 1)
+        def _():
+            y_forward(step1[f], flipped, sa3.at[f])
+            send_below(f, sa3.at[f], d3, 3 + f, 3)
+
 
     arrived(d3, 3)
     x_stage(d3, sa4, tables, flipped, spec_c.at[1], spec_s.at[1], v_ref, g_ref, w_ref)
@@ -314,7 +322,6 @@
 
 def per_device(flight_fields, top_fields, slowness, ref_slowness, flight_blocks, top_block):
     hbm = pl.BlockSpec(memory_space=pltpu.HBM)
-    smem = pl.BlockSpec(memory_space=pltpu.SMEM)
     vmem = pl.BlockSpec(memory_space=pltpu.VMEM)
     pairs = (2, 2 * ROWS, N)
     planes = (2, CHIPS, ROWS, 128)
@@ -322,7 +329,7 @@
     image, after_second = pl.pallas_call(
         kernel,
         out_shape=(jax.ShapeDtypeStruct((ROWS, N), f32), jax.ShapeDtypeStruct(pairs, bf16)),
-        in_specs=[hbm] * 5 + [smem] * 3,
+        in_specs=[hbm] * 6,
         out_specs=(vmem, vmem),
         scratch_shapes=[
             pltpu.VMEM((4, 2 * Q, Q), bf16),
@@ -347,22 +354,26 @@
             pltpu.VMEM((2, N, 128), f32),
             pltpu.VMEM((2, ROWS, N), f32),
             pltpu.VMEM((2, ROWS, N), f32),
-            pltpu.SemaphoreType.DMA((5,)),
+            pltpu.SMEM((DEPTH + 2,), f32),
+            pltpu.SemaphoreType.DMA((6,)),
             pltpu.SemaphoreType.DMA((6,)),
             pltpu.SemaphoreType.DMA((6,)),
             pltpu.SemaphoreType.REGULAR,
         ],
-        compiler_params=pltpu.CompilerParams(collective_id=0, has_side_effects=True, vmem_limit_bytes=60 << 20),
+        compiler_params=pltpu.CompilerParams(collective_id=0, has_side_effects=True, vmem_limit_bytes=48 << 20),
         name="continuation",
     )(
-        jnp.asarray(stacked),
-        jnp.asarray(flipped),
-        flight_fields.reshape(pairs),
-        top_fields.reshape(pairs),
-        slowness.reshape(ROWS, N),
-        ref_slowness,
-        flight_blocks,
-        top_block,
+        *(
+            pltpu.with_memory_space_constraint(value, pltpu.HBM)
+            for value in (
+                jnp.asarray(stacked),
+                jnp.asarray(flipped),
+                flight_fields.reshape(pairs),
+                top_fields.reshape(pairs),
+                slowness.reshape(ROWS, N),
+                jnp.concatenate([flight_blocks.astype(f32), top_block.astype(f32), ref_slowness]),
+            )
+        ),
     )
     return image[None], after_second.reshape(1, 2, 2, ROWS, N)
 

time: 77.1 us -> 73.2 us (0.949)
  the two profiles are of different devices: /device:TPU:1 before, /device:TPU:7 now
where the time goes in v4:
time: 73.2 us; the launch traced here: 73 us
  Pallas kernels  68.5 us (94%)
  local copies, waits for them, and re-layouts  2.01 us (3%)
  between operations  1.94 us (3%)
    pallas_call x1, Pallas kernels, per_device(): pl.pallas_call(kernel, out_shape=(jax.ShapeDtypeStruct((ROWS, N), f32), j...  68.5 us
    unnamed x4, local copies, waits for them, and re-layouts  2.01 us

profile of v4, /device:TPU:7, one launch (start us, length us, event | category | flops | bytes accessed | tf_op | source)
XLA Modules:
  0.0 73.0 jit_solution(13479114389694498842)
XLA Ops:
  1.9 0.0 copy-start
  1.9 0.6 copy-done
  2.6 0.6 pad_maximum_fusion.scalars_hbm
  3.2 68.5 %continuation.1 = (f32[32,1024]{1,0:T(8,128)S(1)}, bf16[2,64,1024]{2,1,0:T(8,128)(2,1)S(1)}) custom-call(bf16[4,512,256]{2,1,0:T(8,128)(2,1)} %constant.4.clone.tables_hbm, bf16[4,512,256]{2,1,0:T(8,128)(2,1)} %constant.5.clone.flipped_hbm, bf16[2,64,1024]{2,1,0:T(8,128)(2,1)} %bitcast.7, bf16[2,64,1024]{2,1,0:T(8,128)(2,1)} %bitcast.8, f32[32,1024]{1,0:T(8,128)} %bitcast.9, ...), custom_call_target="tpu_custom_call" | custom-call | tf_op jit(solution)/shard_map/continuation/pallas_call | solution.py:329
  71.7 0.7 copy.14
  72.3 0.7 copy.15
  (1 shorter events, 0.0 us)
Async XLA Ops:
  1.9 0.7 copy-start

commit v5 on v4

--- a/solution.py
+++ b/solution.py
@@ -162,12 +162,12 @@
 
 
 def kernel(
-    tables_hbm, flipped_hbm, flight_hbm, top_hbm, slow_hbm, scalars_hbm,
+    tables_hbm, flipped_hbm, flight_hbm, top_hbm, slow_hbm, blocks_hbm, ref_s, top_block,
     image, next_fields,
     tables, flipped, flight, top, slow, first_image,
     d1, d3, e2, e4, sa1, sa2, sa3, sa4, step1,
     v_ref, g_ref, w_ref, spec_c, spec_s, rot_c, rot_s,
-    scalars, load_sem, send_sem, recv_sem, entered,
+    flight_blocks, load_sem, send_sem, recv_sem, entered,
 ):
     s = lax.axis_index("depth")
     t = lax.axis_index("trans")
@@ -177,7 +177,7 @@
     loads = [
         pltpu.make_async_copy(src, dst, load_sem.at[i])
         for i, (src, dst) in enumerate(
-            ((flight_hbm, flight), (flipped_hbm, flipped), (slow_hbm, slow), (tables_hbm, tables), (top_hbm, top), (scalars_hbm, scalars))
+            ((flight_hbm, flight), (flipped_hbm, flipped), (slow_hbm, slow), (tables_hbm, tables), (top_hbm, top), (blocks_hbm, flight_blocks))
         )
     ]
     for load in loads[:2]:
@@ -201,17 +201,23 @@
             device_id=(dd, tt), device_id_type=MESH,
         ).start()
 
-    def other_chip(j):
-        m = (j + 1) // 2
-        return lax.rem(chip + 8 + (1 - 2 * lax.rem(j, 2)) * m, CHIPS)
+    def nth_chip(j):
+        half, i = j // 8, lax.rem(j, 8)
+        odd = lax.rem(half + chip, 2)
+        way = 1 - 2 * lax.rem(i, 2)
+        offset = 8 + (1 - odd) * way * 2 * ((i + 1) // 2) - odd * way * (1 + 2 * (i // 2))
+        return lax.rem(chip + offset, CHIPS)
 
     place = pl.ds(pl.multiple_of(t * ROWS, ROWS), ROWS)
 
     def send_cols(f, src, dst, sem_s, sem_r):
-        @pl.loop(0, CHIPS - 1)
+        @pl.loop(0, CHIPS)
         def _(j):
-            q = other_chip(j)
-            remote(src.at[q], dst.at[place], sem_s, sem_r, s, 2 * q + f)
+            q = nth_chip(j)
+
+            @pl.when(q != chip)
+            def _():
+                remote(src.at[q], dst.at[place], sem_s, sem_r, s, 2 * q + f)
 
         @pl.when(core == f)
         def _():
@@ -234,17 +240,20 @@
     def send_below(f, src, dst, sem_s, sem_r):
         @pl.loop(0, CHIPS)
         def _(j):
-            q = other_chip(j)
+            q = nth_chip(j)
             remote(src.at[q], dst.at[place], sem_s, sem_r, below, 2 * q + f)
 
     def send_rows(src, dst, sem_s, sem_r):
-        @pl.loop(0, CHIPS - 1)
+        @pl.loop(0, CHIPS)
         def _(j):
-            q = other_chip(j)
-            for c in range(2):
-                p = 2 * q + c
-                rows = pl.ds(pl.multiple_of(p * ROWS, ROWS), ROWS)
-                remote(src.at[rows], dst.at[core, chip], sem_s, sem_r + core, s, p)
+            q = nth_chip(j)
+
+            @pl.when(q != chip)
+            def _():
+                for c in range(2):
+                    p = 2 * q + c
+                    rows = pl.ds(pl.multiple_of(p * ROWS, ROWS), ROWS)
+                    remote(src.at[rows], dst.at[core, chip], sem_s, sem_r + core, s, p)
 
         pltpu.make_async_copy(src.at[place], dst.at[core, chip], recv_sem.at[sem_r + core]).start()
         p = 2 * chip + 1 - core
@@ -275,12 +284,12 @@
             y_forward(top[f], flipped, sa3.at[f])
             send_below(f, sa3.at[f], d3, 3 + f, 3)
 
-    reference_s = scalars[DEPTH + 1]
+    reference_s = ref_s[0]
     sign = jnp.where(core == 0, 1.0, -1.0)
-    first = scalars[s]
-    second = jnp.where(s == 0, scalars[DEPTH], scalars[jnp.maximum(s - 1, 0)])
+    first = flight_blocks[s]
+    second = jnp.where(s == 0, top_block[0], flight_blocks[jnp.maximum(s - 1, 0)])
     for step, block in enumerate((first, second)):
-        angular = omega_top * (block + 1.0) / NFREQ
+        angular = omega_top * (block.astype(f32) + 1.0) / NFREQ
         spectral(angular, reference_s, chip, sign, spec_c.at[step], spec_s.at[step])
         rotations(angular, reference_s, slow, rot_c.at[step], rot_s.at[step])
     arrived(d1, 0)
@@ -322,6 +331,7 @@
 
 def per_device(flight_fields, top_fields, slowness, ref_slowness, flight_blocks, top_block):
     hbm = pl.BlockSpec(memory_space=pltpu.HBM)
+    smem = pl.BlockSpec(memory_space=pltpu.SMEM)
     vmem = pl.BlockSpec(memory_space=pltpu.VMEM)
     pairs = (2, 2 * ROWS, N)
     planes = (2, CHIPS, ROWS, 128)
@@ -329,7 +339,7 @@
     image, after_second = pl.pallas_call(
         kernel,
         out_shape=(jax.ShapeDtypeStruct((ROWS, N), f32), jax.ShapeDtypeStruct(pairs, bf16)),
-        in_specs=[hbm] * 6,
+        in_specs=[hbm] * 6 + [smem] * 2,
         out_specs=(vmem, vmem),
         scratch_shapes=[
             pltpu.VMEM((4, 2 * Q, Q), bf16),
@@ -354,7 +364,7 @@
             pltpu.VMEM((2, N, 128), f32),
             pltpu.VMEM((2, ROWS, N), f32),
             pltpu.VMEM((2, ROWS, N), f32),
-            pltpu.SMEM((DEPTH + 2,), f32),
+            pltpu.SMEM((DEPTH,), jnp.int32),
             pltpu.SemaphoreType.DMA((6,)),
             pltpu.SemaphoreType.DMA((6,)),
             pltpu.SemaphoreType.DMA((6,)),
@@ -371,9 +381,11 @@
                 flight_fields.reshape(pairs),
                 top_fields.reshape(pairs),
                 slowness.reshape(ROWS, N),
-                jnp.concatenate([flight_blocks.astype(f32), top_block.astype(f32), ref_slowness]),
+                flight_blocks,
             )
         ),
+        ref_slowness,
+        top_block,
     )
     return image[None], after_second.reshape(1, 2, 2, ROWS, N)
 

time: 73.2 us -> 71.3 us (0.974)
  Pallas kernels: 68.5 us -> 67.5 us
    pallas_call x1, Pallas kernels: 68.5 us -> 67.5 us  [per_device(): pl.pallas_call(kernel, out_shape=(jax.ShapeDtypeStruct((ROWS, N), f32), j...]
    unnamed x4 -> x2, local copies, waits for them, and re-layouts: 2.01 us -> 1.36 us
where the time goes in v5:
time: 71.3 us; the launch traced here: 70.8 us
  Pallas kernels  67.5 us (95%)
  between operations  1.93 us (3%)
  local copies, waits for them, and re-layouts  1.36 us (2%)
    pallas_call x1, Pallas kernels, per_device(): pl.pallas_call(kernel, out_shape=(jax.ShapeDtypeStruct((ROWS, N), f32), j...  67.5 us

profile of v5, /device:TPU:7, one launch (start us, length us, event | category | flops | bytes accessed | tf_op | source)
XLA Modules:
  0.0 70.8 jit_solution(8652678325184673370)
XLA Ops:
  1.9 67.5 %continuation.1 = (f32[32,1024]{1,0:T(8,128)S(1)}, bf16[2,64,1024]{2,1,0:T(8,128)(2,1)S(1)}) custom-call(bf16[4,512,256]{2,1,0:T(8,128)(2,1)} %constant.4.clone.tables_hbm, bf16[4,512,256]{2,1,0:T(8,128)(2,1)} %constant.5.clone.flipped_hbm, bf16[2,64,1024]{2,1,0:T(8,128)(2,1)} %bitcast.7, bf16[2,64,1024]{2,1,0:T(8,128)(2,1)} %bitcast.8, f32[32,1024]{1,0:T(8,128)} %bitcast.9, ...), custom_call_target="tpu_custom_call" | custom-call | tf_op jit(solution)/shard_map/continuation/pallas_call | solution.py:339
  69.4 0.7 copy.14
  70.1 0.7 copy.15

commit v6 on v5

--- a/solution.py
+++ b/solution.py
@@ -243,17 +243,28 @@
             q = nth_chip(j)
             remote(src.at[q], dst.at[place], sem_s, sem_r, below, 2 * q + f)
 
-    def send_rows(src, dst, sem_s, sem_r):
+    def send_rows(src, dst, sem_s, sem_r, early):
+        def to_chip(q):
+            for c in range(2):
+                p = 2 * q + c
+                rows = pl.ds(pl.multiple_of(p * ROWS, ROWS), ROWS)
+                remote(src.at[rows], dst.at[core, chip], sem_s, sem_r + core, s, p)
+
+        if early:
+
+            @pl.loop(0, early)
+            def _(q):
+                @pl.when(q != chip)
+                def _():
+                    to_chip(q)
+
         @pl.loop(0, CHIPS)
         def _(j):
             q = nth_chip(j)
 
-            @pl.when(q != chip)
+            @pl.when(jnp.logical_and(q != chip, q >= early))
             def _():
-                for c in range(2):
-                    p = 2 * q + c
-                    rows = pl.ds(pl.multiple_of(p * ROWS, ROWS), ROWS)
-                    remote(src.at[rows], dst.at[core, chip], sem_s, sem_r + core, s, p)
+                to_chip(q)
 
         pltpu.make_async_copy(src.at[place], dst.at[core, chip], recv_sem.at[sem_r + core]).start()
         p = 2 * chip + 1 - core
@@ -294,7 +305,7 @@
         rotations(angular, reference_s, slow, rot_c.at[step], rot_s.at[step])
     arrived(d1, 0)
     x_stage(d1, sa2, tables, flipped, spec_c.at[0], spec_s.at[0], v_ref, g_ref, w_ref)
-    send_rows(sa2, e2, 2, 1)
+    send_rows(sa2, e2, 2, 1, 0)
     for f in range(2):
         arrived(e2.at[f], 1 + f)
         for j, v in enumerate(y_inverse(e2.at[f], tables)):
@@ -312,7 +323,7 @@
 
     arrived(d3, 3)
     x_stage(d3, sa4, tables, flipped, spec_c.at[1], spec_s.at[1], v_ref, g_ref, w_ref)
-    send_rows(sa4, e4, 5, 4)
+    send_rows(sa4, e4, 5, 4, 2)
     for f in range(2):
         arrived(e4.at[f], 4 + f)
         for j, v in enumerate(y_inverse(e4.at[f], tables)):

time: 71.3 us -> 70.4 us (0.987)
  Pallas kernels: 67.5 us -> 66.5 us
    pallas_call x1, Pallas kernels: 67.5 us -> 66.5 us  [per_device(): pl.pallas_call(kernel, out_shape=(jax.ShapeDtypeStruct((ROWS, N), f32), j...]
where the time goes in v6:
time: 70.4 us; the launch traced here: 69.8 us
  Pallas kernels  66.5 us (94%)
  between operations  1.93 us (3%)
  local copies, waits for them, and re-layouts  1.36 us (2%)
    pallas_call x1, Pallas kernels, per_device(): pl.pallas_call(kernel, out_shape=(jax.ShapeDtypeStruct((ROWS, N), f32), j...  66.5 us

profile of v6, /device:TPU:7, one launch (start us, length us, event | category | flops | bytes accessed | tf_op | source)
XLA Modules:
  0.0 69.8 jit_solution(10537703817723022549)
XLA Ops:
  1.9 66.5 %continuation.1 = (f32[32,1024]{1,0:T(8,128)S(1)}, bf16[2,64,1024]{2,1,0:T(8,128)(2,1)S(1)}) custom-call(bf16[4,512,256]{2,1,0:T(8,128)(2,1)} %constant.4.clone.tables_hbm, bf16[4,512,256]{2,1,0:T(8,128)(2,1)} %constant.5.clone.flipped_hbm, bf16[2,64,1024]{2,1,0:T(8,128)(2,1)} %bitcast.7, bf16[2,64,1024]{2,1,0:T(8,128)(2,1)} %bitcast.8, f32[32,1024]{1,0:T(8,128)} %bitcast.9, ...), custom_call_target="tpu_custom_call" | custom-call | tf_op jit(solution)/shard_map/continuation/pallas_call | solution.py:350
  68.5 0.7 copy.14
  69.1 0.7 %copy.15 = bf16[1,2,2,32,1024]{4,3,2,1,0:T(8,128)(2,1)} copy(bf16[1,2,2,32,1024]{4,3,2,1,0:T(8,128)(2,1)S(1)} %bitcast.5) | data formatting | bytes 524288

commit v7 on v6

--- a/solution.py
+++ b/solution.py
@@ -101,24 +101,29 @@
 
 
 def x_stage(src, dst, tables, flipped, spec_c, spec_s, v_ref, g_ref, w_ref):
+    place = {r: slice(128 * n, 128 * (n + 1)) for n, r in enumerate((0, 2, 1, 3))}
+    products = ((0, slice(0, 128)), (2, slice(128, 256)), (1, slice(256, 512)))
     for i in range(Q // BLOCK):
         rows = slice(BLOCK * i, BLOCK * (i + 1))
         u0, u1, u2, u3 = (src[Q * j + BLOCK * i : Q * j + BLOCK * (i + 1)].astype(f32) for j in range(4))
         a, b, c, d = u0 + u2, u1 + u3, u0 - u2, times_i(u1 - u3)
         for r, v in enumerate((a + b, c - d, a - b, c + d)):
-            v_ref[r, rows] = v.astype(bf16)
-    for r in range(4):
-        out = jnp.dot(tables[r], v_ref[r], preferred_element_type=f32)
-        p, q = out[:Q], out[Q:]
+            v_ref[rows, place[r]] = v.astype(bf16)
+    for r, cols in products:
+        out = jnp.dot(tables[r], v_ref[:, cols], preferred_element_type=f32)
         cosines, sines = spec_c[Q * r : Q * (r + 1)], spec_s[Q * r : Q * (r + 1)]
-        g_ref[r] = (p * cosines + q * sines + times_i(p * sines - q * cosines)).astype(bf16)
-    for r in range(4):
-        w_ref[r] = jnp.dot(flipped[r], g_ref[r], preferred_element_type=f32)
+        p, q = out[:Q, :128], out[Q:, :128]
+        g_ref[:, place[r]] = (p * cosines + q * sines + times_i(p * sines - q * cosines)).astype(bf16)
+        if r == 1:
+            p, q = out[:Q, 128:], out[Q:, 128:]
+            g_ref[:, place[3]] = (p * cosines - q * sines + times_i(p * sines + q * cosines)).astype(bf16)
+    for r, cols in products:
+        w_ref[:, cols] = jnp.dot(flipped[r], g_ref[:, cols], preferred_element_type=f32)
     for i in range(Q // BLOCK):
-        p = [w_ref[r, BLOCK * i : BLOCK * (i + 1)] for r in range(4)]
-        q = [w_ref[r, Q + BLOCK * i : Q + BLOCK * (i + 1)] for r in range(4)]
+        p = [w_ref[BLOCK * i : BLOCK * (i + 1), place[r]] for r in range(4)]
+        q = [w_ref[Q + BLOCK * i : Q + BLOCK * (i + 1), place[r]] for r in range(4)]
         pa, pb, pc, pd = p[0] + p[2], p[1] + p[3], p[0] - p[2], p[1] - p[3]
-        qa, qb, qc, qd = q[0] + q[2], q[1] + q[3], q[0] - q[2], q[1] - q[3]
+        qa, qb, qc, qd = q[0] + q[2], q[1] - q[3], q[0] - q[2], q[1] + q[3]
         pairs = ((pa + pb, qa + qb), (pc - qd, qc + pd), (pa - pb, qa - qb), (pc + qd, qc - pd))
         for j, (re, im) in enumerate(pairs):
             dst[Q * j + BLOCK * i : Q * j + BLOCK * (i + 1)] = (re + times_i(im)).astype(bf16)
@@ -129,7 +134,7 @@
     lanes = lax.broadcasted_iota(jnp.int32, (1, 128), 1)
     wave_y = wavenumber(4 * (HALF * lax.rem(chip, 4) + lax.rem(lanes, 64)) + chip // 4)
 
-    @pl.loop(0, N // BLOCK)
+    @pl.loop(0, 3 * Q // BLOCK)
     def _(i):
         start = pl.multiple_of(i * BLOCK, BLOCK)
         r, first = i // (Q // BLOCK), lax.rem(i, Q // BLOCK) * BLOCK
@@ -185,12 +190,12 @@
 
     barrier = pltpu.get_barrier_semaphore()
 
+    for neighbour in (below, above):
+        pl.semaphore_signal(barrier, inc=1, device_id=(neighbour, t), device_id_type=MESH)
+
     @pl.loop(1, TRANS)
     def _(i):
-        pl.semaphore_signal(barrier, inc=1, device_id=(s, lax.rem(t + i, TRANS)), device_id_type=MESH)
-
-    for neighbour in (below, above):
-        pl.semaphore_signal(barrier, inc=1, device_id=(neighbour, t), device_id_type=MESH)
+        pl.semaphore_signal(barrier, inc=1, device_id=(s, lax.rem(t + TRANS - i, TRANS)), device_id_type=MESH)
 
     for load in loads[2:]:
         load.start()
@@ -338,6 +343,14 @@
         sent(sa3.at[f], 3 + f)
     for src, sem in ((sa2, 2), (sa4, 5)):
         sent(src.at[pl.ds(0, N - ROWS)], sem)
+
+
+def store(image, fields, image_out, fields_out, sems):
+    copies = [pltpu.make_async_copy(image, image_out, sems.at[0]), pltpu.make_async_copy(fields, fields_out, sems.at[1])]
+    for copy in copies:
+        copy.start()
+    for copy in copies:
+        copy.wait()
 
 
 def per_device(flight_fields, top_fields, slowness, ref_slowness, flight_blocks, top_block):
@@ -368,11 +381,11 @@
             pltpu.VMEM(planes, bf16),
             pltpu.VMEM((N, 128), bf16),
             pltpu.VMEM(pairs, bf16),
-            pltpu.VMEM((4, Q, 128), bf16),
-            pltpu.VMEM((4, Q, 128), bf16),
-            pltpu.VMEM((4, 2 * Q, 128), f32),
-            pltpu.VMEM((2, N, 128), f32),
-            pltpu.VMEM((2, N, 128), f32),
+            pltpu.VMEM((Q, 512), bf16),
+            pltpu.VMEM((Q, 512), bf16),
+            pltpu.VMEM((2 * Q, 512), f32),
+            pltpu.VMEM((2, 3 * Q, 128), f32),
+            pltpu.VMEM((2, 3 * Q, 128), f32),
             pltpu.VMEM((2, ROWS, N), f32),
             pltpu.VMEM((2, ROWS, N), f32),
             pltpu.SMEM((DEPTH,), jnp.int32),
@@ -398,6 +411,16 @@
         ref_slowness,
         top_block,
     )
+    out = pl.BlockSpec(memory_space=pltpu.HBM)
+    image, after_second = pl.pallas_call(
+        store,
+        out_shape=(jax.ShapeDtypeStruct((ROWS, N), f32), jax.ShapeDtypeStruct(pairs, bf16)),
+        in_specs=[vmem, vmem],
+        out_specs=(out, out),
+        scratch_shapes=[pltpu.SemaphoreType.DMA((2,))],
+        compiler_params=pltpu.CompilerParams(vmem_limit_bytes=2 << 20),
+        name="store",
+    )(image, after_second)
     return image[None], after_second.reshape(1, 2, 2, ROWS, N)
 
 

time: 70.4 us -> 69.9 us (level)
  local copies, waits for them, and re-layouts: 1.36 us -> 0 us
  Pallas kernels: 66.5 us -> 67.8 us
    unnamed x2 -> x0, local copies, waits for them, and re-layouts: 1.36 us -> none
    pallas_call x0 -> x1, Pallas kernels: none -> 0.77 us  [per_device(): pl.pallas_call(store, out_shape=(jax.ShapeDtypeStruct((ROWS, N), f32), ja...]
where the time goes in v7:
time: 69.9 us; the launch traced here: 69.8 us
  Pallas kernels  67.8 us (97%)
  between operations  1.93 us (3%)
    pallas_call x1, Pallas kernels, per_device(): pl.pallas_call(kernel, out_shape=(jax.ShapeDtypeStruct((ROWS, N), f32), j...  67.1 us

profile of v7, /device:TPU:7, one launch (start us, length us, event | category | flops | bytes accessed | tf_op | source)
XLA Modules:
  0.0 69.8 jit_solution(4125916580219604588)
XLA Ops:
  1.9 67.1 %continuation.1 = (f32[32,1024]{1,0:T(8,128)S(1)}, bf16[2,64,1024]{2,1,0:T(8,128)(2,1)S(1)}) custom-call(bf16[4,512,256]{2,1,0:T(8,128)(2,1)} %constant.4.clone.tables_hbm, bf16[4,512,256]{2,1,0:T(8,128)(2,1)} %constant.5.clone.flipped_hbm, bf16[2,64,1024]{2,1,0:T(8,128)(2,1)} %bitcast.5, bf16[2,64,1024]{2,1,0:T(8,128)(2,1)} %bitcast.6, f32[32,1024]{1,0:T(8,128)} %bitcast.7, ...), custom_call_target="tpu_custom_call" | custom-call | tf_op jit(solution)/shard_map/continuation/pallas_call | solution.py:363
  69.0 0.8 %store.1 = (f32[32,1024]{1,0:T(8,128)}, bf16[2,64,1024]{2,1,0:T(8,128)(2,1)}) custom-call(f32[32,1024]{1,0:T(8,128)S(1)} %get-tuple-element.6.image, bf16[2,64,1024]{2,1,0:T(8,128)(2,1)S(1)} %get-tuple-element.7.fields), custom_call_target="tpu_custom_call" | custom-call | tf_op jit(solution)/shard_map/store/pallas_call | solution.py:415

commit v8 on v7

--- a/solution.py
+++ b/solution.py
@@ -328,7 +328,7 @@
 
     arrived(d3, 3)
     x_stage(d3, sa4, tables, flipped, spec_c.at[1], spec_s.at[1], v_ref, g_ref, w_ref)
-    send_rows(sa4, e4, 5, 4, 2)
+    send_rows(sa4, e4, 5, 4, 3)
     for f in range(2):
         arrived(e4.at[f], 4 + f)
         for j, v in enumerate(y_inverse(e4.at[f], tables)):

time: 69.9 us -> 69.9 us (level)
  no operation moved by 1% of the time
where the time goes in v8:
time: 69.9 us; the launch traced here: 69.7 us
  Pallas kernels  67.8 us (97%)
  between operations  1.93 us (3%)
    pallas_call x1, Pallas kernels, per_device(): pl.pallas_call(kernel, out_shape=(jax.ShapeDtypeStruct((ROWS, N), f32), j...  67 us

profile of v8, /device:TPU:7, one launch (start us, length us, event | category | flops | bytes accessed | tf_op | source)
XLA Modules:
  0.0 69.7 jit_solution(708294538548895825)
XLA Ops:
  1.9 67.0 %continuation.1 = (f32[32,1024]{1,0:T(8,128)S(1)}, bf16[2,64,1024]{2,1,0:T(8,128)(2,1)S(1)}) custom-call(bf16[4,512,256]{2,1,0:T(8,128)(2,1)} %constant.4.clone.tables_hbm, bf16[4,512,256]{2,1,0:T(8,128)(2,1)} %constant.5.clone.flipped_hbm, bf16[2,64,1024]{2,1,0:T(8,128)(2,1)} %bitcast.5, bf16[2,64,1024]{2,1,0:T(8,128)(2,1)} %bitcast.6, f32[32,1024]{1,0:T(8,128)} %bitcast.7, ...), custom_call_target="tpu_custom_call" | custom-call | tf_op jit(solution)/shard_map/continuation/pallas_call | solution.py:363
  69.0 0.8 %store.1 = (f32[32,1024]{1,0:T(8,128)}, bf16[2,64,1024]{2,1,0:T(8,128)(2,1)}) custom-call(f32[32,1024]{1,0:T(8,128)S(1)} %get-tuple-element.6.image, bf16[2,64,1024]{2,1,0:T(8,128)(2,1)S(1)} %get-tuple-element.7.fields), custom_call_target="tpu_custom_call" | custom-call | tf_op jit(solution)/shard_map/store/pallas_call | solution.py:415
